TPU v7x, 512 devices: a whole 4x4x16 slice. The times are simulated.
512 devices in a mesh: row: 16 (over z), col: 32 (over y, x, core).
Axes of the slice: x: 4, y: 4, z: 16, core: 2. Of those that a mesh axis runs over, the one named last changes fastest.
Arguments:
- ancestor_inverse: float32 [16384, 16384], P('row', 'col'), may hold values from -6 to 6
- panel_one: bfloat16 [16384, 256], P(('row', 'col')), may hold values from -0.046875 to 0.046875
- panel_two: bfloat16 [16384, 256], P(('row', 'col')), may hold values from -0.046875 to 0.046875
- panel_three: bfloat16 [16384, 256], P(('row', 'col')), may hold values from -0.046875 to 0.046875
- couplings: bfloat16 [3, 256, 256], replicated, may hold values from -0.375 to 0.375
- diag_terms: float32 [3, 256, 256], replicated, may hold values from -6 to 6
- list_two: int32 [60], replicated, may hold values from 0 to 63, as said below
- list_three: int32 [56], replicated, may hold values from 0 to 63, as said below
Outputs:
- inverse_one: float32 [16384, 256], P(('row', 'col'))
- inverse_two: float32 [16384, 256], P(('row', 'col'))
- inverse_three: float32 [16384, 256], P(('row', 'col'))
- small_blocks: float32 [6, 256, 256], P(None, 'row', 'col')
Inputs may be any that keep to these rules, and one draw needn't show every extreme that they name: `list_two`: 60 distinct block indices in increasing order, always including 0 and 63. `list_three`: 56 distinct entries of list_two in increasing order, always including 0 and 63.
All inputs are finite; a program needn't handle non-finite values.
Results may differ from a plain program's by a relative error of at most 0.0003.
Values may be sent and summed in bfloat16 or wider, within the bound.
A program may use at most 64 MiB of HBM per device.

v0:
```python
import jax
import jax.numpy as jnp
from jax import lax
from jax.sharding import Mesh
from jax.sharding import PartitionSpec as P

COL = ("col_0", "col_1", "col_2")
ROW_COL = ("row", "col_0", "col_1", "col_2")


def copy_for_each(value, axis):
    devices = lax.axis_size(axis)
    return lax.all_to_all(
        jnp.broadcast_to(value[None], (devices, *value.shape)), axis, 0, 0, tiled=True
    )


def laid_out(parts, dim):
    parts = jnp.moveaxis(parts, 0, dim)
    shape = parts.shape
    return parts.reshape(*shape[:dim], shape[dim] * shape[dim + 1], *shape[dim + 2 :])


def gathered_by_axis(value, axes, dim):
    far, near = axes
    initial = copy_for_each(value, far)
    parts = jnp.swapaxes(copy_for_each(initial, near), 0, 1)
    return laid_out(parts.reshape(-1, *value.shape), dim)


def from_root(value, axis, root):
    return lax.dynamic_index_in_dim(lax.all_gather(value, axis), root, 0, keepdims=False)


def split_up(value, dim, devices):
    before, after = (value.shape[:dim], value.shape[dim + 1 :])
    return jnp.moveaxis(value.reshape(*before, devices, -1, *after), dim, 0)


def sum_at_owner(value, axis, dim):
    devices = lax.axis_size(axis)
    parts = lax.all_to_all(split_up(value, dim, devices), axis, 0, 0, tiled=True)
    return jnp.sum(parts, axis=0)


def summed_rows(value, axes, dim):
    far, near = axes
    parts = split_up(value, dim, lax.axis_size(far))
    nearer = sum_at_owner(parts, near, dim + 1)
    arrived = lax.all_to_all(nearer, far, split_axis=0, concat_axis=0, tiled=True)
    return arrived.sum(axis=0)


def rows_for(lines, devices):
    spare = -lines.shape[0] % devices
    if not spare:
        return lines
    return jnp.concatenate([lines, jnp.zeros((spare, *lines.shape[1:]), lines.dtype)])


def nested_sum(value, axes):
    padded = rows_for(value, lax.axis_size(axes[0]) * lax.axis_size(axes[1]))
    whole = gathered_by_axis(summed_rows(padded, axes, 0), axes, 0)
    return lax.slice_in_dim(whole, 0, len(value)).reshape(value.shape)


def in_one(arrays, axis):
    ends = [0]
    for a in arrays:
        ends.append(ends[-1] + a.size)
    so_far = nested_sum(jnp.concatenate([a.ravel() for a in arrays]), axis)
    return tuple((so_far[b:e].reshape(a.shape) for a, b, e in zip(arrays, ends, ends[1:])))


def product(former, latter):
    return jnp.dot(
        former, latter, precision=lax.Precision.HIGHEST, preferred_element_type=jnp.float32
    )


def inner_product(former, latter):
    return lax.dot_general(
        former,
        latter,
        (((0,), (0,)), ((), ())),
        precision=lax.Precision.HIGHEST,
        preferred_element_type=jnp.float32,
    )


def piece_keep(listed, start_row, slab_rows, block_width):
    rows_here = start_row + jnp.arange(slab_rows, dtype=jnp.int32)
    matches = (rows_here // block_width)[:, None] == listed[None, :]
    return jnp.any(matches, axis=1).astype(jnp.float32)[:, None]


def spread_joint(own_piece, local_cols):
    rows_all = gathered_by_axis(own_piece, (("col_0", "col_1"), "col_2"), 0)
    col_ratio = lax.axis_size(COL) // lax.axis_size("row")
    col_id = lax.axis_index(COL)
    own_part = lax.dynamic_slice_in_dim(rows_all, col_id % col_ratio * local_cols, local_cols, 0)
    return from_root(own_part, "row", col_id // col_ratio)


def body(
    ancestor_inverse, panel_one, panel_two, panel_three, couplings, diag_terms, list_two, list_three
):
    block_width = couplings.shape[1]
    slab_rows = panel_one.shape[0]
    local_cols = ancestor_inverse.shape[1]
    start_row = (lax.axis_index("row") * lax.axis_size(COL) + lax.axis_index(COL)) * slab_rows
    keep_two = piece_keep(list_two, start_row, slab_rows, block_width)
    keep_three = piece_keep(list_three, start_row, slab_rows, block_width)
    own_two = jnp.where(keep_two > 0.5, panel_two, jnp.zeros_like(panel_two))
    own_three = jnp.where(keep_three > 0.5, panel_three, jnp.zeros_like(panel_three))
    factor_one = panel_one.astype(jnp.float32)
    factor_two = own_two.astype(jnp.float32)
    factor_three = own_three.astype(jnp.float32)
    coupled = couplings.astype(jnp.float32)
    own_all = jnp.concatenate([panel_one, own_two, own_three], axis=1)
    cols_all = spread_joint(own_all, local_cols)
    partial_all = product(ancestor_inverse, cols_all.astype(jnp.float32))
    summed = summed_rows(partial_all, (("col_0", "col_1"), "col_2"), 0)
    sum_one = summed[:, :block_width]
    sum_two = summed[:, block_width : 2 * block_width]
    sum_three = summed[:, 2 * block_width :]
    blocks = (
        inner_product(factor_one, sum_one),
        inner_product(factor_two, sum_one),
        inner_product(factor_two, sum_two),
        inner_product(factor_three, sum_one),
        inner_product(factor_three, sum_two),
        inner_product(factor_three, sum_three),
    )
    m_oneone, m_twoone, m_twotwo, m_threeone, m_threetwo, m_threethree = in_one(
        (blocks[0], blocks[1], blocks[2], blocks[3], blocks[4], blocks[5]),
        (("row", "col_0"), ("col_1", "col_2")),
    )
    inverse_one = -sum_one
    inverse_two = -(sum_two - product(sum_one, coupled[0])) * keep_two
    inverse_three = (
        -(sum_three + product(inverse_one, coupled[1]) + product(inverse_two, coupled[2]))
        * keep_three
    )
    diag_one = diag_terms[0] + m_oneone
    cross_two = m_twoone.T - product(diag_one, coupled[0])
    diag_two = (
        diag_terms[1]
        + m_twotwo
        - product(m_twoone, coupled[0])
        - inner_product(coupled[0], cross_two)
    )
    second_three = m_threetwo - product(m_threeone, coupled[0])
    cross_first = -(-m_threeone.T + product(diag_one, coupled[1]) + product(cross_two, coupled[2]))
    cross_second = -(
        -second_three.T + inner_product(cross_two, coupled[1]) + product(diag_two, coupled[2])
    )
    diag_three = (
        diag_terms[2]
        + m_threethree
        - product(m_threeone, coupled[1])
        - product(second_three, coupled[2])
        - inner_product(coupled[1], cross_first)
        - inner_product(coupled[2], cross_second)
    )
    stacked = jnp.stack([diag_one, diag_two, diag_three, cross_two, cross_first, cross_second])
    tile_rows = block_width // lax.axis_size("row")
    tile_cols = block_width // lax.axis_size(COL)
    own_tile = lax.dynamic_slice(
        stacked,
        (0, lax.axis_index("row") * tile_rows, lax.axis_index(COL) * tile_cols),
        (6, tile_rows, tile_cols),
    )
    return (inverse_one, inverse_two, inverse_three, own_tile)


def solution(mesh):
    split = Mesh(
        mesh.devices.reshape(mesh.shape["row"], 4, 4, 2), ("row", "col_0", "col_1", "col_2")
    )
    return jax.shard_map(
        body,
        mesh=split,
        in_specs=(
            P("row", COL),
            P(ROW_COL, None),
            P(ROW_COL, None),
            P(ROW_COL, None),
            P(),
            P(),
            P(),
            P(),
        ),
        out_specs=(P(ROW_COL, None), P(ROW_COL, None), P(ROW_COL, None), P(None, "row", COL)),
        check_vma=False,
    )
```

profile of v0, /device:TPU:1, one launch (start us, length us, event | category | flops | bytes accessed | tf_op | source)
XLA Modules:
  0.0 398.7 jit_solution(6740270312410938486)
XLA Ops:
  11.6 7.6 %all-to-all-start = ((bf16[16,32,768]{2,1,0:T(8,128)(2,1)}), bf16[16,32,768]{2,1,0:T(8,128)(2,1)S(1)}, u32[]{:S(2)}, u32[]{:S(2)}) async-start(bf16[16,32,768]{2,1,0:T(8,128)(2,1)} %broadcast_in_dim.25), calls=%async_computation | async-start | bytes 1572864 | tf_op jit(solution)/shard_map/all_to_all | solution.py:13
  19.2 11.7 %all-to-all-done = bf16[16,32,768]{2,1,0:T(8,128)(2,1)S(1)} async-done(((bf16[16,32,768]{2,1,0:T(8,128)(2,1)}), bf16[16,32,768]{2,1,0:T(8,128)(2,1)S(1)}, u32[]{:S(2)}, u32[]{:S(2)}) %all-to-all-start) | async-done | bytes 786464 | tf_op jit(solution)/shard_map/all_to_all | solution.py:13
  31.1 8.2 %all_to_all.45 = bf16[2,16,32,768]{3,2,1,0:T(8,128)(2,1)S(1)} all-to-all(bf16[2,16,32,768]{3,2,1,0:T(8,128)(2,1)S(1)} %broadcast_in_dim.26), channel_id=1, replica_groups=mesh['row'=16,'col_0'=4,'col_1'=4,'col_2'=2] {'col_2'}, dimensions={0} | all-to-all | bytes 3145728 | tf_op jit(solution)/shard_map/all_to_all | solution.py:13
  40.5 148.0 %all-gather.3.cloned.1.call-done = bf16[8192,768]{1,0:T(8,128)(2,1)} async-done(((bf16[512,768]{1,0:T(8,128)(2,1)}), bf16[8192,768]{1,0:T(8,128)(2,1)}) %all-gather.3.cloned.1.call-update) | async-done | bytes 12582928 | tf_op jit(solution)/shard_map/all_gather | solution.py:32
  188.5 5.8 %convolution_bitcast_fusion = f32[1024,768]{0,1:T(8,128)} fusion(f32[1024,512]{1,0:T(8,128)S(1)} %copy-done, bf16[16,512,768]{2,1,0:T(8,128)(2,1)} %bitcast.140, s32[]{:T(128)S(6)} %select_n.47), kind=kOutput, calls=%fused_computation | convolution fusion | flops 4831838208 | bytes 6029316 | tf_op jit(solution)/shard_map/dot_general | solution.py:76
  194.2 3.5 copy.54
  197.7 2.2 copy.55
  200.0 7.7 %all_to_all.46 = f32[2,16,32,768]{3,2,1,0:T(8,128)} all-to-all(f32[2,16,32,768]{3,2,1,0:T(8,128)S(1)} %copy.55), channel_id=1, replica_groups=mesh['row'=16,'col_0'=4,'col_1'=4,'col_2'=2] {'col_2'}, dimensions={0} | all-to-all | bytes 6291456 | tf_op jit(solution)/shard_map/all_to_all | solution.py:42
  207.7 3.4 reduce_sum.36
  211.1 28.6 %all_to_all.47 = f32[16,32,768]{2,1,0:T(8,128)} all-to-all(f32[16,32,768]{2,1,0:T(8,128)} %reduce_sum.36), channel_id=1, replica_groups=mesh['row'=16,'col_0'=4,'col_1'=4,'col_2'=2] {'col_0','col_1'}, dimensions={0} | all-to-all | bytes 3145728 | tf_op jit(solution)/shard_map/all_to_all | solution.py:50
  239.7 1.5 reduce_sum.37
  244.5 1.8 copy.56
  246.3 1.1 copy.71
  247.4 1.1 copy.72
  253.3 2.6 reshape_reshape.12
  255.9 1.9 copy.57
  257.8 25.5 %all_to_all.48 = f32[8,64,768]{2,1,0:T(8,128)} all-to-all(f32[8,64,768]{2,1,0:T(8,128)S(1)} %copy.57), channel_id=1, replica_groups=mesh['row'=16,'col_0'=4,'col_1'=4,'col_2'=2] {'col_1','col_2'}, dimensions={0} | all-to-all | bytes 3145728 | tf_op jit(solution)/shard_map/all_to_all | solution.py:42
  283.3 1.5 reduce_sum.38
  284.9 26.6 %all_to_all.49 = f32[64,1,768]{2,1,0:T(1,128)S(1)} all-to-all(f32[64,1,768]{2,1,0:T(1,128)S(1)} %all_to_all.33), channel_id=1, replica_groups=mesh['row'=16,'col_0'=4,'col_1'=4,'col_2'=2] {'row','col_0'}, dimensions={0} | all-to-all | bytes 393216 | tf_op jit(solution)/shard_map/all_to_all | solution.py:50
  311.8 23.4 %all_to_all.50 = f32[64,1,768]{2,1,0:T(1,128)S(1)} all-to-all(f32[64,1,768]{2,1,0:T(1,128)S(1)} %broadcast_in_dim.27), channel_id=1, replica_groups=mesh['row'=16,'col_0'=4,'col_1'=4,'col_2'=2] {'row','col_0'}, dimensions={0} | all-to-all | bytes 393216 | tf_op jit(solution)/shard_map/all_to_all | solution.py:13
  335.2 1.3 broadcast_in_dim.51
  336.5 9.0 %all-to-all-start.7 = ((f32[8,64,768]{2,1,0:T(8,128)}), f32[8,64,768]{2,1,0:T(8,128)}, u32[]{:S(2)}, u32[]{:S(2)}) async-start(f32[8,64,768]{2,1,0:T(8,128)} %broadcast_in_dim.51), calls=%async_computation.7 | async-start | bytes 3145728 | tf_op jit(solution)/shard_map/all_to_all | solution.py:13
  347.1 19.0 %all-to-all-done.7 = f32[8,64,768]{2,1,0:T(8,128)} async-done(((f32[8,64,768]{2,1,0:T(8,128)}), f32[8,64,768]{2,1,0:T(8,128)}, u32[]{:S(2)}, u32[]{:S(2)}) %all-to-all-start.7) | async-done | bytes 1572896 | tf_op jit(solution)/shard_map/all_to_all | solution.py:13
  366.1 3.5 copy.58
  369.6 2.7 slice.72
  372.3 1.4 convolution_subtract_fusion.1
  373.8 1.4 convolution_subtract_fusion.3
  375.1 1.4 convolution_add_fusion.3
  378.6 1.8 copy.59
  380.4 2.1 convolution_subtract_fusion.4
  382.5 1.8 copy.64
  390.4 1.4 constant_dynamic-slice_fusion
  (70 shorter events, 24.0 us)
Async XLA Ops:
  7.2 181.3 %copy-start = (f32[1024,512]{1,0:T(8,128)S(1)}, f32[1024,512]{1,0:T(8,128)}, u32[]{:S(2)}) copy-start(f32[1024,512]{1,0:T(8,128)} %param.8) | copy-start | bytes 6291460
  11.6 19.4 %all-to-all-start = ((bf16[16,32,768]{2,1,0:T(8,128)(2,1)}), bf16[16,32,768]{2,1,0:T(8,128)(2,1)S(1)}, u32[]{:S(2)}, u32[]{:S(2)}) async-start(bf16[16,32,768]{2,1,0:T(8,128)(2,1)} %broadcast_in_dim.25), calls=%async_computation | async-start | bytes 1572864 | tf_op jit(solution)/shard_map/all_to_all | solution.py:13
  19.2 169.3 %all-gather.3.cloned.1.call-start = ((), (), s32[]{:S(2)}) async-start(), calls=%async_computation.8 | async-start | bytes 13369344 | tf_op jit(solution)/shard_map/all_gather | solution.py:32
  239.7 1.5 copy-start.7
  336.5 9.0 %copy-start.1 = (bf16[3,256,256]{2,1,0:T(8,128)(2,1)S(1)}, bf16[3,256,256]{2,1,0:T(8,128)(2,1)}, u32[]{:S(2)}) copy-start(bf16[3,256,256]{2,1,0:T(8,128)(2,1)} %param.12) | copy-start | bytes 1179652
  336.5 29.7 %all-to-all-start.7 = ((f32[8,64,768]{2,1,0:T(8,128)}), f32[8,64,768]{2,1,0:T(8,128)}, u32[]{:S(2)}, u32[]{:S(2)}) async-start(f32[8,64,768]{2,1,0:T(8,128)} %broadcast_in_dim.51), calls=%async_computation.7 | async-start | bytes 3145728 | tf_op jit(solution)/shard_map/all_to_all | solution.py:13
  345.4 0.6 copy-start.5
  345.7 0.6 copy-start.6
  369.6 4.1 %copy-start.3 = (f32[3,256,256]{2,1,0:T(8,128)S(1)}, f32[3,256,256]{2,1,0:T(8,128)}, u32[]{:S(2)}) copy-start(f32[3,256,256]{2,1,0:T(8,128)} %param.13) | copy-start | bytes 2359300
  372.3 4.2 %copy-start.2 = (f32[1536,256]{1,0:T(8,128)S(1)}, f32[1536,256]{1,0:T(8,128)}, u32[]{:S(2)}) copy-start(f32[1536,256]{1,0:T(8,128)} %slice.72) | copy-start | bytes 4718596
  384.2 1.4 copy-start.4
  385.9 1.2 copy-start.8
Sparse Core Ops, SparseCore 0:
  40.6 147.8 all-gather.2
where the time goes:
time: 400 us; the launch traced here: 399 us
  waiting for transfers between devices  179 us (45%)
  blocking collectives  120 us (30%)
  local copies, waits for them, and re-layouts  39.3 us (10%)
  matrix products  18.9 us (5%)
  starting transfers between devices  16.6 us (4%)
  between operations  14.4 us (4%)
  other arithmetic  10.8 us (3%)
    all_gather x1, waiting for transfers between devices, from_root(): lax.all_gather(value, axis)  148 us
    all_to_all x2, blocking collectives, summed_rows(): lax.all_to_all(nearer, far, split_axis=0, concat_axis=0, tiled=True)  55.2 us
    all_to_all x2, blocking collectives, sum_at_owner(): lax.all_to_all(split_up(value, dim, devices), axis, 0, 0, tiled=True)  33.2 us
    all_to_all x2, blocking collectives, copy_for_each(): lax.all_to_all(jnp.broadcast_to(value[None], (devices, *value.shape)), ax...  31.6 us
    all_to_all x2, waiting for transfers between devices, copy_for_each(): lax.all_to_all(jnp.broadcast_to(value[None], (devices, *value.shape)), ax...  30.8 us
    all_to_all x2, starting transfers between devices, copy_for_each(): lax.all_to_all(jnp.broadcast_to(value[None], (devices, *value.shape)), ax...  16.5 us
    dot_general x12, matrix products, product(): jnp.dot(former, latter, precision=lax.Precision.HIGHEST, preferred_elemen...  14.4 us
    unnamed x34, local copies, waits for them, and re-layouts  10.7 us
  transfers between devices with their start and end apart: 3, of which 3 were waited for; matrix products, arithmetic and copies ran while one was open for 0% of the time, Pallas kernels for 0%

commit v1 on v0

v1 whole, which is shorter than its diff:
```python
import functools

import jax
import jax.numpy as jnp
from jax import lax
from jax.experimental import pallas as pl
from jax.experimental.pallas import tpu as pltpu
from jax.sharding import PartitionSpec as P

MESH = pl.DeviceIdType.MESH
HI = lax.Precision.HIGHEST
F32 = jnp.float32
BF16 = jnp.bfloat16
NZ, NK, W, ROWS = 16, 16, 256, 32
HALF = 384


def mm(a, b):
    return jnp.dot(a, b, precision=HI, preferred_element_type=F32)


def tmm(a, b):
    return lax.dot_general(a, b, (((0,), (0,)), ((), ())), precision=HI, preferred_element_type=F32)


def keep_of(lines, block):
    return jnp.max(jnp.where(lines == block, 1.0, 0.0).astype(F32))


def kernel(
    a_hbm, p1, p2, p3, coup, diag, l2, l3,
    o1, o2, o3, ot,
    a_vm, ahi, alo, ring, fbuf, pown, ppar, prec,
    xra, yra, xrb, yrb, ra, rb, ysum,
    phi, qrec, x2a, y2a, x2b, y2b, r2a, r2b, zsend, zrec,
    lsem, up_s, up_r, dn_s, dn_r, f_s, f_r, pr_s, pr_r,
    xa_s, xa_r, ya_s, ya_r, xb_s, xb_r, yb_s, yb_r,
    q_s, q_r, x2a_s, x2a_r, y2a_s, y2a_r, x2b_s, x2b_r, y2b_s, y2b_r, z_s, z_r,
):
    z = lax.axis_index("row")
    c = lax.axis_index("col")
    e = c % 2
    k = c // 2
    y = k // 4
    x = k % 4
    half = y // 2
    partner = k * 2 + (1 - e)

    def col_of(yy, xx):
        return (yy * 4 + xx) * 2 + e

    acopy = pltpu.make_async_copy(a_hbm, a_vm, lsem.at[0])
    acopy.start()
    own = []
    for i, p in enumerate((p1, p2, p3)):
        cp = pltpu.make_async_copy(p, ring.at[z, :, pl.ds(i * W, W)], lsem.at[1 + i])
        cp.start()
        own.append(cp)

    barrier = pltpu.get_barrier_semaphore()
    for d in range(1, 32):
        pl.semaphore_signal(barrier, inc=1, device_id=(z, (c + d) % 32), device_id_type=MESH)
    for d in range(1, 16):
        pl.semaphore_signal(barrier, inc=1, device_id=((z + d) % 16, c), device_id_type=MESH)

    lines2 = l2[...]
    lines3 = l3[...]
    block = (z * 32 + c) // 8
    keep2 = keep_of(lines2, block)
    keep3 = keep_of(lines3, block)
    c0 = coup[0].astype(F32)
    c1 = coup[1].astype(F32)
    c2 = coup[2].astype(F32)
    first = jnp.where((z == 0) & (c == 0), 1.0, 0.0).astype(F32)
    g1 = diag[0]
    h21 = -mm(g1, c0)
    g2 = diag[1] - tmm(c0, h21)
    h31 = -(mm(g1, c1) + mm(h21, c2))
    h32 = -(tmm(h21, c1) + mm(g2, c2))
    g3 = diag[2] - tmm(c1, h31) - tmm(c2, h32)
    for i, v in enumerate((g1, g2, g3, h21, h31, h32)):
        phi[i] = (v.T * first).reshape(4, 4, 2, 8, W)

    acopy.wait()

    @pl.loop(0, 16)
    def _(i):
        v = a_vm[pl.ds(pl.multiple_of(i * 64, 64), 64), :]
        hi = v.astype(BF16)
        ahi[i] = hi.reshape(2, 32, 512)
        alo[i] = (v - hi.astype(F32)).astype(BF16).reshape(2, 32, 512)

    for cp in own:
        cp.wait()
    pl.semaphore_wait(barrier, 46)

    up, down = (z + 1) % 16, (z + 15) % 16
    slot = (k % 8) * 2 + e

    def ring_copy(item, s, send, recv, to):
        return pltpu.make_async_remote_copy(
            src_ref=ring.at[item], dst_ref=ring.at[item], send_sem=send.at[s], recv_sem=recv.at[s],
            device_id=(to, c), device_id_type=MESH)

    def plane_copy(item):
        return pltpu.make_async_remote_copy(
            src_ref=ring.at[item], dst_ref=fbuf.at[slot], send_sem=f_s.at[item], recv_sem=f_r.at[slot],
            device_id=(z, item * 2 + half), device_id_type=MESH)

    def spread(item):
        mine = (item * 2 + half) == c

        @pl.when(mine)
        def _():
            pltpu.make_async_copy(ring.at[item], fbuf.at[slot], f_r.at[slot]).start()

        @pl.when(jnp.logical_not(mine))
        def _():
            plane_copy(item).start()

    ring_copy(z, 0, up_s, up_r, up).start()
    ring_copy(z, 0, dn_s, dn_r, down).start()
    spread(z)
    for s in range(1, 9):
        item = (z + 16 - s) % 16
        ring_copy(item, s - 1, up_s, up_r, up).wait_recv()
        if s < 8:
            ring_copy(item, s, up_s, up_r, up).start()
        spread(item)
        if s < 8:
            item = (z + s) % 16
            ring_copy(item, s - 1, dn_s, dn_r, down).wait_recv()
            if s < 7:
                ring_copy(item, s, dn_s, dn_r, down).start()
            spread(item)

    f1 = ring[z, :, 0:W].astype(F32)
    f2 = ring[z, :, W:2 * W].astype(F32) * keep2
    f3 = ring[z, :, 2 * W:3 * W].astype(F32) * keep3
    b = mm(f1, c0)
    g = mm(f1, c1)
    h = mm(f2, c2)
    q = mm(b, c2)

    for i in range(16):
        pltpu.make_async_copy(ring.at[i], fbuf.at[i], f_r.at[i]).wait()
    for j in range(2):
        s8 = slice(8 * j, 8 * j + 8)
        m2 = keep_of(lines2, 2 * c + j)
        m3 = keep_of(lines3, 2 * c + j)
        fbuf[s8, :, W:2 * W] = (fbuf[s8, :, W:2 * W].astype(F32) * m2).astype(BF16)
        fbuf[s8, :, 2 * W:3 * W] = (fbuf[s8, :, 2 * W:3 * W].astype(F32) * m3).astype(BF16)

    def part(side, cols):
        f = fbuf[:, :, cols].reshape(512, HALF)
        out = jnp.dot(ahi[:, side].reshape(512, 512), f, preferred_element_type=F32)
        out = out + jnp.dot(alo[:, side].reshape(512, 512), f, preferred_element_type=F32)
        return out.reshape(4, 4, ROWS, HALF)

    alpha, beta = slice(0, HALF), slice(HALF, 2 * HALF)
    pair = []
    for i, cols in enumerate((alpha, beta)):
        ppar[:, :, :, cols] = part(1 - e, cols)
        cp = pltpu.make_async_remote_copy(
            src_ref=ppar.at[:, :, :, cols], dst_ref=prec.at[:, :, :, cols],
            send_sem=pr_s.at[i], recv_sem=pr_r.at[i], device_id=(z, partner), device_id_type=MESH)
        cp.start()
        pair.append(cp)
    for cols in (alpha, beta):
        pown[:, :, :, cols] = part(e, cols)

    def exchange(src, rec, send, recv, d, to):
        cp = pltpu.make_async_remote_copy(
            src_ref=src, dst_ref=rec.at[d - 1], send_sem=send.at[d - 1], recv_sem=recv.at[d - 1],
            device_id=(z, to), device_id_type=MESH)
        cp.start()
        return cp

    pair[0].wait_recv()
    pown[:, :, :, alpha] += prec[:, :, :, alpha]
    xa = [exchange(pown.at[:, (x + d) % 4, :, alpha], xra, xa_s, xa_r, d, col_of(y, (x + d) % 4))
          for d in (2, 1, 3)]
    pair[1].wait_recv()
    pown[:, :, :, beta] += prec[:, :, :, beta]
    xb = [exchange(pown.at[(y + d) % 4, :, :, beta], xrb, xb_s, xb_r, d, col_of((y + d) % 4, x))
          for d in (2, 1, 3)]
    for cp in xa:
        cp.wait_recv()
    ra[...] = pown[:, x, :, alpha] + xra[0] + xra[1] + xra[2]
    ya = [exchange(ra.at[(y + d) % 4], yra, ya_s, ya_r, d, col_of((y + d) % 4, x)) for d in (2, 1, 3)]
    for cp in xb:
        cp.wait_recv()
    rb[...] = pown[y, :, :, beta] + xrb[0] + xrb[1] + xrb[2]
    yb = [exchange(rb.at[(x + d) % 4], yrb, yb_s, yb_r, d, col_of(y, (x + d) % 4)) for d in (2, 1, 3)]
    for cp in ya:
        cp.wait_recv()
    ysum[:, alpha] = ra[y] + yra[0] + yra[1] + yra[2]
    for cp in yb:
        cp.wait_recv()
    ysum[:, beta] = rb[x] + yrb[0] + yrb[1] + yrb[2]

    y1 = ysum[:, 0:W]
    a = mm(y1, c0)
    w = mm(y1, c1)
    y2 = (ysum[:, W:2 * W] - a) * keep2
    v = mm(y2, c2)
    u = mm(a, c2)
    y3 = (ysum[:, 2 * W:3 * W] - w - v) * keep3
    o1[...] = -y1
    o2[...] = -y2
    o3[...] = -y3

    def add(i, right, left):
        val = tmm(jnp.concatenate(right, axis=0), jnp.concatenate(left, axis=0))
        phi[i] += val.reshape(4, 4, 2, 8, W)

    add(0, [y1], [f1])
    add(3, [f2, -a], [y1, f1])
    add(1, [y2, -f2, a], [f2, a, b])
    add(4, [f3 - h, u - w], [y1, f1])
    add(5, [f3, -(w + v), g + h, -u], [y2, f2, a, b])
    add(2, [y3, h - f3, w - u, -f3, w + v, -(g + h), u], [f3, w, g, v, h, u, q])

    qc = pltpu.make_async_remote_copy(
        src_ref=phi.at[:, :, :, 1 - e], dst_ref=qrec,
        send_sem=q_s.at[0], recv_sem=q_r.at[0], device_id=(z, partner), device_id_type=MESH)
    qc.start()
    qc.wait_recv()
    qrec[...] += phi[:, :, :, e]
    s2a = [exchange(qrec.at[0:3, :, (x + d) % 4], x2a, x2a_s, x2a_r, d, col_of(y, (x + d) % 4))
           for d in (2, 1, 3)]
    s2b = [exchange(qrec.at[3:6, (y + d) % 4], x2b, x2b_s, x2b_r, d, col_of((y + d) % 4, x))
           for d in (2, 1, 3)]
    for cp in s2a:
        cp.wait_recv()
    r2a[...] = qrec[0:3, :, x] + x2a[0] + x2a[1] + x2a[2]
    t2a = [exchange(r2a.at[:, (y + d) % 4], y2a, y2a_s, y2a_r, d, col_of((y + d) % 4, x)) for d in (2, 1, 3)]
    for cp in s2b:
        cp.wait_recv()
    r2b[...] = qrec[3:6, y] + x2b[0] + x2b[1] + x2b[2]
    t2b = [exchange(r2b.at[:, (x + d) % 4], y2b, y2b_s, y2b_r, d, col_of(y, (x + d) % 4)) for d in (2, 1, 3)]
    for cp in t2a:
        cp.wait_recv()
    sa = r2a[:, y] + y2a[0] + y2a[1] + y2a[2]
    for cp in t2b:
        cp.wait_recv()
    sb = r2b[:, x] + y2b[0] + y2b[1] + y2b[2]

    for zz in range(16):
        for i in range(6):
            src = sa[i] if i < 3 else sb[i - 3]
            zsend[zz, :, 16 * i:16 * i + 16] = src[:, 16 * zz:16 * zz + 16]
        zsend[zz, :, 96:128] = jnp.zeros((8, 32), F32)
    zc = []
    for d in (8, 7, 9, 6, 10, 5, 11, 4, 12, 3, 13, 2, 14, 1, 15):
        to = (z + d) % 16
        cp = pltpu.make_async_remote_copy(
            src_ref=zsend.at[to], dst_ref=zrec.at[d - 1], send_sem=z_s.at[d - 1], recv_sem=z_r.at[d - 1],
            device_id=(to, c), device_id_type=MESH)
        cp.start()
        zc.append(cp)
    for cp in zc:
        cp.wait_recv()
    tile = zsend[z]
    for d in range(15):
        tile = tile + zrec[d]
    turned = tile.T
    for i in range(6):
        ot[i] = turned[16 * i:16 * i + 16, :]

    for s in range(8):
        ring_copy(z, s, up_s, up_r, up).wait_send()
    for s in range(7):
        ring_copy(z, s, dn_s, dn_r, down).wait_send()
    for i in range(16):
        @pl.when((i * 2 + half) != c)
        def _():
            plane_copy(i).wait_send()
    for cp in pair + xa + xb + ya + yb + [qc] + s2a + s2b + t2a + t2b + zc:
        cp.wait_send()


def body(ancestor_inverse, panel_one, panel_two, panel_three, couplings, diag_terms, list_two, list_three):
    any_spec = pl.BlockSpec(memory_space=pl.ANY)
    vm = pl.BlockSpec(memory_space=pltpu.VMEM)
    dma = pltpu.SemaphoreType.DMA
    return pl.pallas_call(
        kernel,
        out_shape=(
            jax.ShapeDtypeStruct((ROWS, W), F32),
            jax.ShapeDtypeStruct((ROWS, W), F32),
            jax.ShapeDtypeStruct((ROWS, W), F32),
            jax.ShapeDtypeStruct((6, 16, 8), F32),
        ),
        in_specs=[any_spec] * 4 + [vm] * 4,
        out_specs=(vm,) * 4,
        scratch_shapes=[
            pltpu.VMEM((1024, 512), F32),
            pltpu.VMEM((16, 2, 32, 512), BF16),
            pltpu.VMEM((16, 2, 32, 512), BF16),
            pltpu.VMEM((16, ROWS, 768), BF16),
            pltpu.VMEM((16, ROWS, 768), BF16),
            pltpu.VMEM((4, 4, ROWS, 768), F32),
            pltpu.VMEM((4, 4, ROWS, 768), F32),
            pltpu.VMEM((4, 4, ROWS, 768), F32),
            pltpu.VMEM((3, 4, ROWS, HALF), F32),
            pltpu.VMEM((3, ROWS, HALF), F32),
            pltpu.VMEM((3, 4, ROWS, HALF), F32),
            pltpu.VMEM((3, ROWS, HALF), F32),
            pltpu.VMEM((4, ROWS, HALF), F32),
            pltpu.VMEM((4, ROWS, HALF), F32),
            pltpu.VMEM((ROWS, 768), F32),
            pltpu.VMEM((6, 4, 4, 2, 8, W), F32),
            pltpu.VMEM((6, 4, 4, 8, W), F32),
            pltpu.VMEM((3, 3, 4, 8, W), F32),
            pltpu.VMEM((3, 3, 8, W), F32),
            pltpu.VMEM((3, 3, 4, 8, W), F32),
            pltpu.VMEM((3, 3, 8, W), F32),
            pltpu.VMEM((3, 4, 8, W), F32),
            pltpu.VMEM((3, 4, 8, W), F32),
            pltpu.VMEM((16, 8, 128), F32),
            pltpu.VMEM((15, 8, 128), F32),
            dma((4,)), dma((8,)), dma((8,)), dma((7,)), dma((7,)), dma((16,)), dma((16,)), dma((2,)), dma((2,)),
            dma((3,)), dma((3,)), dma((3,)), dma((3,)), dma((3,)), dma((3,)), dma((3,)), dma((3,)),
            dma((1,)), dma((1,)), dma((3,)), dma((3,)), dma((3,)), dma((3,)), dma((3,)), dma((3,)),
            dma((3,)), dma((3,)), dma((15,)), dma((15,)),
        ],
        compiler_params=pltpu.CompilerParams(
            collective_id=0, has_side_effects=True, vmem_limit_bytes=56 << 20
        ),
        name="chain_inverse",
    )(
        ancestor_inverse, panel_one, panel_two, panel_three, couplings, diag_terms,
        list_two.reshape(1, -1), list_three.reshape(1, -1),
    )


def solution(mesh):
    rows = P(("row", "col"), None)
    return jax.shard_map(
        body,
        mesh=mesh,
        in_specs=(P("row", "col"), rows, rows, rows, P(), P(), P(), P()),
        out_specs=(rows, rows, rows, P(None, "row", "col")),
        check_vma=False,
    )
```

time: 400 us -> 103 us (0.26)
  waiting for transfers between devices: 179 us -> 0 us
  blocking collectives: 120 us -> 0 us
  Pallas kernels: 0 us -> 96.2 us
  local copies, waits for them, and re-layouts: 39.3 us -> 5.6 us
  matrix products: 18.9 us -> 0 us
  starting transfers between devices: 16.6 us -> 0 us
  between operations: 14.4 us -> 0.64 us
  other arithmetic: 10.8 us -> 0 us
    all_gather x1 -> x0, waiting for transfers between devices: 148 us -> none  [from_root(): lax.all_gather(value, axis)]
    all_to_all x6 -> x0, blocking collectives: 120 us -> none  [the longest x2 55.2 us: summed_rows(): lax.all_to_all(nearer, far, split_axis=0, concat_axis=0, tiled=True)]
    pallas_call x0 -> x1, Pallas kernels: none -> 96.2 us  [body(): pl.pallas_call(kernel, out_shape=(jax.ShapeDtypeStruct((ROWS, W), F32), j...]
    all_to_all x2 -> x0, waiting for transfers between devices: 30.8 us -> none  [copy_for_each(): lax.all_to_all(jnp.broadcast_to(value[None], (devices, *value.shape)), ax...]
    dot_general x22 -> x0, matrix products: 18.9 us -> none  [the longest x12 14.4 us: product(): jnp.dot(former, latter, precision=lax.Precision.HIGHEST, preferred_elemen...]
    all_to_all x2 -> x0, starting transfers between devices: 16.5 us -> none  [copy_for_each(): lax.all_to_all(jnp.broadcast_to(value[None], (devices, *value.shape)), ax...]
    transpose x3 -> x0, local copies, waits for them, and re-layouts: 7.6 us -> none  [the longest x2 4.12 us: split_up(): return jnp.moveaxis(value.reshape(*before, devices, -1, *after), dim, 0)]
    reduce_sum x4 -> x0, other arithmetic: 6.58 us -> none  [the longest x2 4.93 us: sum_at_owner(): return jnp.sum(parts, axis=0)]
  transfers between devices with their start and end apart: 3 -> 0, of which waited for: 3 -> 0; matrix products, arithmetic and copies ran while one was open for 0% -> 0% of each run, Pallas kernels for 0% -> 0%
where the time goes in v1:
time: 103 us; the launch traced here: 102 us
  Pallas kernels  96.2 us (93%)
  local copies, waits for them, and re-layouts  5.6 us (5%)
    pallas_call x1, Pallas kernels, body(): pl.pallas_call(kernel, out_shape=(jax.ShapeDtypeStruct((ROWS, W), F32), j...  96.2 us
    unnamed x3, local copies, waits for them, and re-layouts  4.12 us

profile of v1, /device:TPU:1, one launch (start us, length us, event | category | flops | bytes accessed | tf_op | source)
XLA Modules:
  0.0 102.4 jit_solution(15123982022171115468)
XLA Ops:
  0.6 96.2 %chain_inverse.1 = (f32[32,256]{1,0:T(8,128)}, f32[32,256]{1,0:T(8,128)}, f32[32,256]{1,0:T(8,128)}, f32[6,16,8]{2,1,0:T(8,128)}) custom-call(f32[1024,512]{1,0:T(8,128)} %a_hbm.1, bf16[32,256]{1,0:T(8,128)(2,1)} %p1.1, bf16[32,256]{1,0:T(8,128)(2,1)} %p2.1, bf16[32,256]{1,0:T(8,128)(2,1)} %p3.1, bf16[3,256,256]{2,1,0:T(8,128)(2,1)} %coup.1, ...), custom_call_target="tpu_custom_call" | custom-call | tf_op jit(solution)/shard_map/chain_inverse/pallas_call | solution.py:287
  96.8 1.5 %copy.12 = f32[6,16,8]{1,2,0:T(8,128)} copy(f32[6,16,8]{2,1,0:T(8,128)} %get-tuple-element.7) | data formatting | bytes 6144 | tf_op jit(solution)/shard_map/chain_inverse/pallas_call | solution.py:287
  98.3 1.4 %copy.16 = f32[32,256]{1,0:T(8,128)} copy(f32[32,256]{1,0:T(8,128)} %get-tuple-element.12) | data formatting | bytes 65536
  99.7 1.4 %copy.17 = f32[32,256]{1,0:T(8,128)} copy(f32[32,256]{1,0:T(8,128)} %get-tuple-element.13) | data formatting | bytes 65536
  101.0 1.4 %copy.18 = f32[32,256]{1,0:T(8,128)} copy(f32[32,256]{1,0:T(8,128)} %get-tuple-element.14) | data formatting | bytes 65536

commit v2 on v1

--- a/solution.py
+++ b/solution.py
@@ -29,7 +29,7 @@
 
 def kernel(
     a_hbm, p1, p2, p3, coup, diag, l2, l3,
-    o1, o2, o3, ot,
+    o, ot,
     a_vm, ahi, alo, ring, fbuf, pown, ppar, prec,
     xra, yra, xrb, yrb, ra, rb, ysum,
     phi, qrec, x2a, y2a, x2b, y2b, r2a, r2b, zsend, zrec,
@@ -60,8 +60,54 @@
     barrier = pltpu.get_barrier_semaphore()
     for d in range(1, 32):
         pl.semaphore_signal(barrier, inc=1, device_id=(z, (c + d) % 32), device_id_type=MESH)
-    for d in range(1, 16):
+    for d in (1, 15):
         pl.semaphore_signal(barrier, inc=1, device_id=((z + d) % 16, c), device_id_type=MESH)
+
+    for cp in own:
+        cp.wait()
+    pl.semaphore_wait(barrier, 33)
+
+    up, down = (z + 1) % 16, (z + 15) % 16
+    slot = (k % 8) * 2 + e
+
+    def ring_copy(item, s, q, send, recv, to):
+        part = ring.at[item, :, pl.ds(q * W, W)]
+        return pltpu.make_async_remote_copy(
+            src_ref=part, dst_ref=part, send_sem=send.at[3 * s + q], recv_sem=recv.at[3 * s + q],
+            device_id=(to, c), device_id_type=MESH)
+
+    def plane_copy(item):
+        return pltpu.make_async_remote_copy(
+            src_ref=ring.at[item], dst_ref=fbuf.at[slot], send_sem=f_s.at[item], recv_sem=f_r.at[slot],
+            device_id=(z, item * 2 + half), device_id_type=MESH)
+
+    def spread(item):
+        mine = (item * 2 + half) == c
+
+        @pl.when(mine)
+        def _():
+            pltpu.make_async_copy(ring.at[item], fbuf.at[slot], f_r.at[slot]).start()
+
+        @pl.when(jnp.logical_not(mine))
+        def _():
+            plane_copy(item).start()
+
+    for q in range(3):
+        ring_copy(z, 0, q, up_s, up_r, up).start()
+        ring_copy(z, 0, q, dn_s, dn_r, down).start()
+    spread(z)
+    for s in range(1, 9):
+        below, above = (z + 16 - s) % 16, (z + s) % 16
+        for q in range(3):
+            ring_copy(below, s - 1, q, up_s, up_r, up).wait_recv()
+            if s < 8:
+                ring_copy(below, s, q, up_s, up_r, up).start()
+                ring_copy(above, s - 1, q, dn_s, dn_r, down).wait_recv()
+            if s < 7:
+                ring_copy(above, s, q, dn_s, dn_r, down).start()
+        spread(below)
+        if s < 8:
+            spread(above)
 
     lines2 = l2[...]
     lines3 = l3[...]
@@ -90,58 +136,6 @@
         ahi[i] = hi.reshape(2, 32, 512)
         alo[i] = (v - hi.astype(F32)).astype(BF16).reshape(2, 32, 512)
 
-    for cp in own:
-        cp.wait()
-    pl.semaphore_wait(barrier, 46)
-
-    up, down = (z + 1) % 16, (z + 15) % 16
-    slot = (k % 8) * 2 + e
-
-    def ring_copy(item, s, send, recv, to):
-        return pltpu.make_async_remote_copy(
-            src_ref=ring.at[item], dst_ref=ring.at[item], send_sem=send.at[s], recv_sem=recv.at[s],
-            device_id=(to, c), device_id_type=MESH)
-
-    def plane_copy(item):
-        return pltpu.make_async_remote_copy(
-            src_ref=ring.at[item], dst_ref=fbuf.at[slot], send_sem=f_s.at[item], recv_sem=f_r.at[slot],
-            device_id=(z, item * 2 + half), device_id_type=MESH)
-
-    def spread(item):
-        mine = (item * 2 + half) == c
-
-        @pl.when(mine)
-        def _():
-            pltpu.make_async_copy(ring.at[item], fbuf.at[slot], f_r.at[slot]).start()
-
-        @pl.when(jnp.logical_not(mine))
-        def _():
-            plane_copy(item).start()
-
-    ring_copy(z, 0, up_s, up_r, up).start()
-    ring_copy(z, 0, dn_s, dn_r, down).start()
-    spread(z)
-    for s in range(1, 9):
-        item = (z + 16 - s) % 16
-        ring_copy(item, s - 1, up_s, up_r, up).wait_recv()
-        if s < 8:
-            ring_copy(item, s, up_s, up_r, up).start()
-        spread(item)
-        if s < 8:
-            item = (z + s) % 16
-            ring_copy(item, s - 1, dn_s, dn_r, down).wait_recv()
-            if s < 7:
-                ring_copy(item, s, dn_s, dn_r, down).start()
-            spread(item)
-
-    f1 = ring[z, :, 0:W].astype(F32)
-    f2 = ring[z, :, W:2 * W].astype(F32) * keep2
-    f3 = ring[z, :, 2 * W:3 * W].astype(F32) * keep3
-    b = mm(f1, c0)
-    g = mm(f1, c1)
-    h = mm(f2, c2)
-    q = mm(b, c2)
-
     for i in range(16):
         pltpu.make_async_copy(ring.at[i], fbuf.at[i], f_r.at[i]).wait()
     for j in range(2):
@@ -176,21 +170,53 @@
         cp.start()
         return cp
 
+    def relay(view, rec, send, recv, p, right, left):
+        def go(ref, n, to):
+            cp = pltpu.make_async_remote_copy(
+                src_ref=ref, dst_ref=rec.at[n], send_sem=send.at[n], recv_sem=recv.at[n],
+                device_id=(z, to), device_id_type=MESH)
+            cp.start()
+            return cp
+
+        far, after, before = (p + 2) % 4, (p + 1) % 4, (p + 3) % 4
+        cps = [go(view(far, 0), 0, right), go(view(far, 1), 1, left),
+               go(view(after, 1), 2, right), go(view(before, 0), 3, left)]
+
+        def middle():
+            for n, q, h, to in ((0, after, 0, right), (1, before, 1, left)):
+                cps[n].wait_recv()
+                ref = view(q, h)
+                ref[...] += rec[n]
+                cps.append(go(ref, 4 + n, to))
+
+        def finish():
+            for cp in cps[2:]:
+                cp.wait_recv()
+            return view(p, 0)[...] + rec[3] + rec[4], view(p, 1)[...] + rec[2] + rec[5]
+
+        return cps, middle, finish
+
+    xn, yn = [col_of(y, (x + d) % 4) for d in (1, 3)], [col_of((y + d) % 4, x) for d in (1, 3)]
     pair[0].wait_recv()
     pown[:, :, :, alpha] += prec[:, :, :, alpha]
-    xa = [exchange(pown.at[:, (x + d) % 4, :, alpha], xra, xa_s, xa_r, d, col_of(y, (x + d) % 4))
-          for d in (2, 1, 3)]
+    xa, xa_mid, xa_end = relay(lambda q, h: pown.at[2 * h:2 * h + 2, q, :, alpha], xra, xa_s, xa_r, x, *xn)
     pair[1].wait_recv()
     pown[:, :, :, beta] += prec[:, :, :, beta]
-    xb = [exchange(pown.at[(y + d) % 4, :, :, beta], xrb, xb_s, xb_r, d, col_of((y + d) % 4, x))
-          for d in (2, 1, 3)]
-    for cp in xa:
-        cp.wait_recv()
-    ra[...] = pown[:, x, :, alpha] + xra[0] + xra[1] + xra[2]
+    xb, xb_mid, xb_end = relay(lambda q, h: pown.at[q, 2 * h:2 * h + 2, :, beta], xrb, xb_s, xb_r, y, *yn)
+    xa_mid()
+    xb_mid()
+
+    f1 = ring[z, :, 0:W].astype(F32)
+    f2 = ring[z, :, W:2 * W].astype(F32) * keep2
+    f3 = ring[z, :, 2 * W:3 * W].astype(F32) * keep3
+    b = mm(f1, c0)
+    g = mm(f1, c1)
+    h = mm(f2, c2)
+    q = mm(b, c2)
+
+    ra[0:2], ra[2:4] = xa_end()
     ya = [exchange(ra.at[(y + d) % 4], yra, ya_s, ya_r, d, col_of((y + d) % 4, x)) for d in (2, 1, 3)]
-    for cp in xb:
-        cp.wait_recv()
-    rb[...] = pown[y, :, :, beta] + xrb[0] + xrb[1] + xrb[2]
+    rb[0:2], rb[2:4] = xb_end()
     yb = [exchange(rb.at[(x + d) % 4], yrb, yb_s, yb_r, d, col_of(y, (x + d) % 4)) for d in (2, 1, 3)]
     for cp in ya:
         cp.wait_recv()
@@ -206,9 +232,9 @@
     v = mm(y2, c2)
     u = mm(a, c2)
     y3 = (ysum[:, 2 * W:3 * W] - w - v) * keep3
-    o1[...] = -y1
-    o2[...] = -y2
-    o3[...] = -y3
+    o[0] = -y1
+    o[1] = -y2
+    o[2] = -y3
 
     def add(i, right, left):
         val = tmm(jnp.concatenate(right, axis=0), jnp.concatenate(left, axis=0))
@@ -227,17 +253,15 @@
     qc.start()
     qc.wait_recv()
     qrec[...] += phi[:, :, :, e]
-    s2a = [exchange(qrec.at[0:3, :, (x + d) % 4], x2a, x2a_s, x2a_r, d, col_of(y, (x + d) % 4))
-           for d in (2, 1, 3)]
-    s2b = [exchange(qrec.at[3:6, (y + d) % 4], x2b, x2b_s, x2b_r, d, col_of((y + d) % 4, x))
-           for d in (2, 1, 3)]
-    for cp in s2a:
-        cp.wait_recv()
-    r2a[...] = qrec[0:3, :, x] + x2a[0] + x2a[1] + x2a[2]
+    s2a, s2a_mid, s2a_end = relay(
+        lambda q, h: qrec.at[0:3, 2 * h:2 * h + 2, q], x2a, x2a_s, x2a_r, x, *xn)
+    s2b, s2b_mid, s2b_end = relay(
+        lambda q, h: qrec.at[3:6, q, 2 * h:2 * h + 2], x2b, x2b_s, x2b_r, y, *yn)
+    s2a_mid()
+    s2b_mid()
+    r2a[:, 0:2], r2a[:, 2:4] = s2a_end()
     t2a = [exchange(r2a.at[:, (y + d) % 4], y2a, y2a_s, y2a_r, d, col_of((y + d) % 4, x)) for d in (2, 1, 3)]
-    for cp in s2b:
-        cp.wait_recv()
-    r2b[...] = qrec[3:6, y] + x2b[0] + x2b[1] + x2b[2]
+    r2b[:, 0:2], r2b[:, 2:4] = s2b_end()
     t2b = [exchange(r2b.at[:, (x + d) % 4], y2b, y2b_s, y2b_r, d, col_of(y, (x + d) % 4)) for d in (2, 1, 3)]
     for cp in t2a:
         cp.wait_recv()
@@ -264,14 +288,13 @@
     tile = zsend[z]
     for d in range(15):
         tile = tile + zrec[d]
-    turned = tile.T
-    for i in range(6):
-        ot[i] = turned[16 * i:16 * i + 16, :]
-
-    for s in range(8):
-        ring_copy(z, s, up_s, up_r, up).wait_send()
-    for s in range(7):
-        ring_copy(z, s, dn_s, dn_r, down).wait_send()
+    ot[...] = tile
+
+    for q in range(3):
+        for s in range(8):
+            ring_copy(z, s, q, up_s, up_r, up).wait_send()
+        for s in range(7):
+            ring_copy(z, s, q, dn_s, dn_r, down).wait_send()
     for i in range(16):
         @pl.when((i * 2 + half) != c)
         def _():
@@ -280,20 +303,26 @@
         cp.wait_send()
 
 
+def hand_out(blocks, tile, o1, o2, o3, ot):
+    o1[...] = blocks[0]
+    o2[...] = blocks[1]
+    o3[...] = blocks[2]
+    for i in range(6):
+        ot[i] = tile[:, 16 * i:16 * i + 16]
+
+
 def body(ancestor_inverse, panel_one, panel_two, panel_three, couplings, diag_terms, list_two, list_three):
     any_spec = pl.BlockSpec(memory_space=pl.ANY)
     vm = pl.BlockSpec(memory_space=pltpu.VMEM)
     dma = pltpu.SemaphoreType.DMA
-    return pl.pallas_call(
+    blocks, tile = pl.pallas_call(
         kernel,
         out_shape=(
-            jax.ShapeDtypeStruct((ROWS, W), F32),
-            jax.ShapeDtypeStruct((ROWS, W), F32),
-            jax.ShapeDtypeStruct((ROWS, W), F32),
-            jax.ShapeDtypeStruct((6, 16, 8), F32),
+            jax.ShapeDtypeStruct((3, ROWS, W), F32),
+            jax.ShapeDtypeStruct((8, 128), F32),
         ),
         in_specs=[any_spec] * 4 + [vm] * 4,
-        out_specs=(vm,) * 4,
+        out_specs=(vm,) * 2,
         scratch_shapes=[
             pltpu.VMEM((1024, 512), F32),
             pltpu.VMEM((16, 2, 32, 512), BF16),
@@ -303,26 +332,26 @@
             pltpu.VMEM((4, 4, ROWS, 768), F32),
             pltpu.VMEM((4, 4, ROWS, 768), F32),
             pltpu.VMEM((4, 4, ROWS, 768), F32),
-            pltpu.VMEM((3, 4, ROWS, HALF), F32),
+            pltpu.VMEM((6, 2, ROWS, HALF), F32),
             pltpu.VMEM((3, ROWS, HALF), F32),
-            pltpu.VMEM((3, 4, ROWS, HALF), F32),
+            pltpu.VMEM((6, 2, ROWS, HALF), F32),
             pltpu.VMEM((3, ROWS, HALF), F32),
             pltpu.VMEM((4, ROWS, HALF), F32),
             pltpu.VMEM((4, ROWS, HALF), F32),
             pltpu.VMEM((ROWS, 768), F32),
             pltpu.VMEM((6, 4, 4, 2, 8, W), F32),
             pltpu.VMEM((6, 4, 4, 8, W), F32),
-            pltpu.VMEM((3, 3, 4, 8, W), F32),
+            pltpu.VMEM((6, 3, 2, 8, W), F32),
             pltpu.VMEM((3, 3, 8, W), F32),
-            pltpu.VMEM((3, 3, 4, 8, W), F32),
+            pltpu.VMEM((6, 3, 2, 8, W), F32),
             pltpu.VMEM((3, 3, 8, W), F32),
             pltpu.VMEM((3, 4, 8, W), F32),
             pltpu.VMEM((3, 4, 8, W), F32),
             pltpu.VMEM((16, 8, 128), F32),
             pltpu.VMEM((15, 8, 128), F32),
-            dma((4,)), dma((8,)), dma((8,)), dma((7,)), dma((7,)), dma((16,)), dma((16,)), dma((2,)), dma((2,)),
-            dma((3,)), dma((3,)), dma((3,)), dma((3,)), dma((3,)), dma((3,)), dma((3,)), dma((3,)),
-            dma((1,)), dma((1,)), dma((3,)), dma((3,)), dma((3,)), dma((3,)), dma((3,)), dma((3,)),
+            dma((4,)), dma((24,)), dma((24,)), dma((21,)), dma((21,)), dma((16,)), dma((16,)), dma((2,)), dma((2,)),
+            dma((6,)), dma((6,)), dma((3,)), dma((3,)), dma((6,)), dma((6,)), dma((3,)), dma((3,)),
+            dma((1,)), dma((1,)), dma((6,)), dma((6,)), dma((3,)), dma((3,)), dma((6,)), dma((6,)),
             dma((3,)), dma((3,)), dma((15,)), dma((15,)),
         ],
         compiler_params=pltpu.CompilerParams(
@@ -333,6 +362,14 @@
         ancestor_inverse, panel_one, panel_two, panel_three, couplings, diag_terms,
         list_two.reshape(1, -1), list_three.reshape(1, -1),
     )
+    *inverses, small = pl.pallas_call(
+        hand_out,
+        out_shape=(jax.ShapeDtypeStruct((ROWS, W), F32),) * 3 + (jax.ShapeDtypeStruct((6, 8, 16), F32),),
+        in_specs=[vm] * 2,
+        out_specs=(vm,) * 4,
+        name="hand_out",
+    )(blocks, tile)
+    return (*inverses, jnp.swapaxes(small, 1, 2))
 
 
 def solution(mesh):

time: 103 us -> 91 us (0.88)
  Pallas kernels: 96.2 us -> 89.3 us
  local copies, waits for them, and re-layouts: 5.6 us -> 0 us
    pallas_call x1 -> x2, Pallas kernels: 96.2 us -> 89.3 us  [the longest x1 87.7 us: body(): pl.pallas_call(kernel, out_shape=(jax.ShapeDtypeStruct((3, ROWS, W), F32)...]
    unnamed x3 -> x0, local copies, waits for them, and re-layouts: 4.12 us -> none
    pallas_call x1 -> x0, local copies, waits for them, and re-layouts: 1.48 us -> none  [body(): pl.pallas_call(kernel, out_shape=(jax.ShapeDtypeStruct((ROWS, W), F32), j...]
where the time goes in v2:
time: 91 us; the launch traced here: 89.9 us
  Pallas kernels  89.3 us (98%)
    pallas_call x1, Pallas kernels, body(): pl.pallas_call(kernel, out_shape=(jax.ShapeDtypeStruct((3, ROWS, W), F32)...  87.7 us

profile of v2, /device:TPU:1, one launch (start us, length us, event | category | flops | bytes accessed | tf_op | source)
XLA Modules:
  0.0 89.9 jit_solution(9088534680280115067)
XLA Ops:
  0.6 87.7 %chain_inverse.1 = (f32[3,32,256]{2,1,0:T(8,128)}, f32[8,128]{1,0:T(8,128)}) custom-call(f32[1024,512]{1,0:T(8,128)} %a_hbm.1, bf16[32,256]{1,0:T(8,128)(2,1)} %p1.1, bf16[32,256]{1,0:T(8,128)(2,1)} %p2.1, bf16[32,256]{1,0:T(8,128)(2,1)} %p3.1, bf16[3,256,256]{2,1,0:T(8,128)(2,1)} %coup.1, f32[3,256,256]{2,1,0:T(8,128)} %diag.1, s32[1,60]{1,0:T(1,128)} %bitcast.3, ...), custom_call_target="tpu_custom_call" | custom-call | tf_op jit(solution)/shard_map/chain_inverse/pallas_call | solution.py:318
  88.4 1.6 %hand_out.1 = (f32[32,256]{1,0:T(8,128)}, f32[32,256]{1,0:T(8,128)}, f32[32,256]{1,0:T(8,128)}, f32[6,8,16]{2,1,0:T(8,128)}) custom-call(f32[3,32,256]{2,1,0:T(8,128)} %get-tuple-element.10.blocks, f32[8,128]{1,0:T(8,128)} %get-tuple-element.11.tile), custom_call_target="tpu_custom_call" | custom-call | tf_op jit(solution)/shard_map/hand_out/pallas_call | solution.py:365

commit v3 on v2

v3 whole, which is shorter than its diff:
```python
import functools

import jax
import jax.numpy as jnp
from jax import lax
from jax.experimental import pallas as pl
from jax.experimental.pallas import tpu as pltpu
from jax.sharding import PartitionSpec as P

MESH = pl.DeviceIdType.MESH
F32 = jnp.float32
BF16 = jnp.bfloat16
NZ, NK, W, ROWS = 16, 16, 256, 32
STREAMS = ((0, 256), (256, 512), (512, 640), (640, 768))


def halves(v):
    hi = v.astype(BF16)
    return hi, (v - hi.astype(F32)).astype(BF16)


def mm(v, c):
    hi, lo = halves(v)
    return jnp.dot(hi, c, preferred_element_type=F32) + jnp.dot(lo, c, preferred_element_type=F32)


def turned_dot(a, b):
    return lax.dot_general(a, b, (((0,), (0,)), ((), ())), preferred_element_type=F32)


def tmc(v, c):
    hi, lo = halves(v)
    return turned_dot(hi, c) + turned_dot(lo, c)


def ctm(c, v):
    hi, lo = halves(v)
    return turned_dot(c, hi) + turned_dot(c, lo)


def tmm(a, b):
    ah, al = halves(a)
    bh, bl = halves(b)
    return turned_dot(jnp.concatenate([ah, al, ah], axis=0), jnp.concatenate([bh, bh, bl], axis=0))


def keep_of(lines, block):
    return jnp.max(jnp.where(lines == block, 1.0, 0.0).astype(F32))


def kernel(
    a_hbm, p1, p2, p3, coup_hbm, diag_hbm, l2, l3,
    o, ot,
    a_vm, coup, diag, ahi, alo, ring, fbuf, pown, ppar, prec,
    rec0, rec1, rec2, rec3, far0, far1, far2, far3, mid0, mid1, mid2, mid3, ysum,
    phi, qrec, x2a, y2a, x2b, y2b, r2a, r2b, zsend, zrec,
    lsem, in_sem, up_s, up_r, dn_s, dn_r, f_s, f_r, pr_s, pr_r,
    rel_s, rel_r, far_s, far_r,
    q_s, q_r, x2a_s, x2a_r, y2a_s, y2a_r, x2b_s, x2b_r, y2b_s, y2b_r, z_s, z_r,
):
    z = lax.axis_index("row")
    c = lax.axis_index("col")
    e = c % 2
    k = c // 2
    y = k // 4
    x = k % 4
    half = y // 2
    partner = k * 2 + (1 - e)

    def col_of(yy, xx):
        return (yy * 4 + xx) * 2 + e

    own = []
    for i, p in enumerate((p1, p2, p3)):
        cp = pltpu.make_async_copy(p, ring.at[z, i], lsem.at[1 + i])
        cp.start()
        own.append(cp)
    acopy = pltpu.make_async_copy(a_hbm, a_vm, lsem.at[0])
    ccopy = pltpu.make_async_copy(coup_hbm, coup, lsem.at[4])
    dcopy = pltpu.make_async_copy(diag_hbm, diag, lsem.at[5])
    for cp in (acopy, ccopy, dcopy):
        cp.start()

    barrier = pltpu.get_barrier_semaphore()
    line = [partner]
    cross = []
    for d in (1, 2, 3):
        for ee in (0, 1):
            line.append((y * 4 + (x + d) % 4) * 2 + ee)
            cross.append(((y + d) % 4 * 4 + x) * 2 + ee)
    for to in line + cross:
        pl.semaphore_signal(barrier, inc=1, device_id=(z, to), device_id_type=MESH)
    for d in (1, 15):
        pl.semaphore_signal(barrier, inc=1, device_id=((z + d) % 16, c), device_id_type=MESH)
    for cp in own:
        cp.wait()
    pl.semaphore_wait(barrier, 15)
    for to in cross:
        pl.semaphore_signal(in_sem, inc=1, device_id=(z, to), device_id_type=MESH)

    up, down = (z + 1) % 16, (z + 15) % 16
    slot = (k % 8) * 2 + e

    def ring_copy(item, s, q, send, recv, to):
        part = ring.at[item, q]
        return pltpu.make_async_remote_copy(
            src_ref=part, dst_ref=part, send_sem=send.at[3 * s + q], recv_sem=recv.at[3 * s + q],
            device_id=(to, c), device_id_type=MESH)

    def plane_copy(item, q):
        return pltpu.make_async_remote_copy(
            src_ref=ring.at[item, q], dst_ref=fbuf.at[q, slot],
            send_sem=f_s.at[3 * item + q], recv_sem=f_r.at[3 * slot + q],
            device_id=(z, item * 2 + half), device_id_type=MESH)

    def spread(item, q):
        mine = (item * 2 + half) == c

        @pl.when(mine)
        def _():
            pltpu.make_async_copy(ring.at[item, q], fbuf.at[q, slot], f_r.at[3 * slot + q]).start()

        @pl.when(jnp.logical_not(mine))
        def _():
            plane_copy(item, q).start()

    for q in range(3):
        ring_copy(z, 0, q, up_s, up_r, up).start()
        ring_copy(z, 0, q, dn_s, dn_r, down).start()
    pl.semaphore_wait(in_sem, 6)
    for q in range(3):
        spread(z, q)
    for s in range(1, 9):
        below, above = (z + 16 - s) % 16, (z + s) % 16
        for q in range(3):
            ring_copy(below, s - 1, q, up_s, up_r, up).wait_recv()
            if s < 8:
                ring_copy(below, s, q, up_s, up_r, up).start()
                ring_copy(above, s - 1, q, dn_s, dn_r, down).wait_recv()
            if s < 7:
                ring_copy(above, s, q, dn_s, dn_r, down).start()
            spread(below, q)
            if s < 8:
                spread(above, q)

    lines2 = l2[...]
    lines3 = l3[...]
    block = (z * 32 + c) // 8
    keep2 = keep_of(lines2, block)
    keep3 = keep_of(lines3, block)
    acopy.wait()

    @pl.loop(0, 16)
    def _(i):
        hi, lo = halves(a_vm[pl.ds(pl.multiple_of(i * 64, 64), 64), :])
        ahi[i] = hi.reshape(2, 32, 512)
        alo[i] = lo.reshape(2, 32, 512)

    ccopy.wait()
    dcopy.wait()
    c0, c1, c2 = coup[0], coup[1], coup[2]
    f1 = ring[z, 0].astype(F32)
    f2 = ring[z, 1].astype(F32) * keep2
    f3 = ring[z, 2].astype(F32) * keep3
    b = mm(f1, c0)
    g = mm(f1, c1)
    h = mm(f2, c2)
    q_ = mm(b, c2)

    def arrived(q):
        for i in range(16):
            pltpu.make_async_copy(ring.at[i, q], fbuf.at[q, i], f_r.at[3 * i + q]).wait()
        if q:
            lines = lines2 if q == 1 else lines3
            for j in range(2):
                s8 = slice(8 * j, 8 * j + 8)
                fbuf[q, s8] = (fbuf[q, s8].astype(F32) * keep_of(lines, 2 * c + j)).astype(BF16)

    def part(side, q):
        f = fbuf[q].reshape(512, W)
        out = jnp.dot(ahi[:, side].reshape(512, 512), f, preferred_element_type=F32)
        out = out + jnp.dot(alo[:, side].reshape(512, 512), f, preferred_element_type=F32)
        return out.reshape(4, 4, ROWS, W)

    def panel(q):
        return pl.ds(q * W, W)

    pair = []

    def to_partner(q):
        ppar[:, :, :, panel(q)] = part(1 - e, q)
        cp = pltpu.make_async_remote_copy(
            src_ref=ppar.at[:, :, :, panel(q)], dst_ref=prec.at[:, :, :, panel(q)],
            send_sem=pr_s.at[q], recv_sem=pr_r.at[q], device_id=(z, partner), device_id_type=MESH)
        cp.start()
        pair.append(cp)

    def from_partner(q):
        pair[q].wait_recv()
        pown[:, :, :, panel(q)] += prec[:, :, :, panel(q)]

    def exchange(src, rec, send, recv, d, to, n=0):
        cp = pltpu.make_async_remote_copy(
            src_ref=src, dst_ref=rec.at[d - 1], send_sem=send.at[n + d - 1], recv_sem=recv.at[n + d - 1],
            device_id=(z, to), device_id_type=MESH)
        cp.start()
        return cp

    def relay(view, rec, send, recv, p, right, left, base=0):
        def go(ref, n, to):
            cp = pltpu.make_async_remote_copy(
                src_ref=ref, dst_ref=rec.at[n], send_sem=send.at[base + n], recv_sem=recv.at[base + n],
                device_id=(z, to), device_id_type=MESH)
            cp.start()
            return cp

        far, after, before = (p + 2) % 4, (p + 1) % 4, (p + 3) % 4
        cps = [go(view(far, 0), 0, right), go(view(far, 1), 1, left),
               go(view(after, 1), 2, right), go(view(before, 0), 3, left)]

        def middle():
            for n, q, h, to in ((0, after, 0, right), (1, before, 1, left)):
                cps[n].wait_recv()
                ref = view(q, h)
                ref[...] += rec[n]
                cps.append(go(ref, 4 + n, to))

        def finish():
            for cp in cps[2:]:
                cp.wait_recv()
            return view(p, 0)[...] + rec[3] + rec[4], view(p, 1)[...] + rec[2] + rec[5]

        return cps, middle, finish

    xn, yn = [col_of(y, (x + d) % 4) for d in (1, 3)], [col_of((y + d) % 4, x) for d in (1, 3)]
    recs, mids, fars = (rec0, rec1, rec2, rec3), (mid0, mid1, mid2, mid3), (far0, far1, far2, far3)
    mid_of, end_of, second = [], [], [[], [], [], []]

    def open_stream(n):
        lo, hi = STREAMS[n]
        if n % 2 == 0:
            r = relay(lambda q, h: pown.at[2 * h:2 * h + 2, q, :, lo:hi], recs[n], rel_s, rel_r, x, *xn, base=6 * n)
        else:
            r = relay(lambda q, h: pown.at[q, 2 * h:2 * h + 2, :, lo:hi], recs[n], rel_s, rel_r, y, *yn, base=6 * n)
        mid_of.append((r[1], r[0]))
        end_of.append(r[2])

    def second_stage(n):
        mids[n][0:2], mids[n][2:4] = end_of[n]()
        for d in (2, 1, 3):
            if n % 2 == 0:
                src, to = mids[n].at[(y + d) % 4], col_of((y + d) % 4, x)
            else:
                src, to = mids[n].at[(x + d) % 4], col_of(y, (x + d) % 4)
            second[n].append(exchange(src, fars[n], far_s, far_r, d, to, n=3 * n))

    def close_stream(n):
        for cp in second[n]:
            cp.wait_recv()
        lo, hi = STREAMS[n]
        own_part = mids[n][y if n % 2 == 0 else x]
        ysum[:, lo:hi] = own_part + fars[n][0] + fars[n][1] + fars[n][2]

    arrived(0)
    to_partner(0)
    pown[:, :, :, panel(0)] = part(e, 0)
    arrived(1)
    to_partner(1)
    from_partner(0)
    open_stream(0)
    pown[:, :, :, panel(1)] = part(e, 1)
    arrived(2)
    to_partner(2)
    from_partner(1)
    open_stream(1)
    pown[:, :, :, panel(2)] = part(e, 2)
    mid_of[0][0]()
    from_partner(2)
    open_stream(2)
    open_stream(3)
    mid_of[1][0]()
    second_stage(0)
    mid_of[2][0]()
    mid_of[3][0]()

    first = jnp.where((z == 0) & (c == 0), 1.0, 0.0).astype(F32)
    g1 = diag[0]
    h21 = -mm(g1, c0)
    g2 = diag[1] - ctm(c0, h21)
    h31 = -(mm(g1, c1) + mm(h21, c2))
    h32 = -(tmc(h21, c1) + mm(g2, c2))
    g3 = diag[2] - ctm(c1, h31) - ctm(c2, h32)
    for i, v in enumerate((g1, g2, g3, h21, h31, h32)):
        phi[i] = (v.T * first).reshape(4, 4, 2, 8, W)

    second_stage(1)
    second_stage(2)
    second_stage(3)
    for n in range(4):
        close_stream(n)

    y1 = ysum[:, 0:W]
    a = mm(y1, c0)
    w = mm(y1, c1)
    y2 = (ysum[:, W:2 * W] - a) * keep2
    v = mm(y2, c2)
    u = mm(a, c2)
    y3 = (ysum[:, 2 * W:3 * W] - w - v) * keep3
    o[0] = -y1
    o[1] = -y2
    o[2] = -y3

    def add(i, right, left):
        val = tmm(jnp.concatenate(right, axis=0), jnp.concatenate(left, axis=0))
        phi[i] += val.reshape(4, 4, 2, 8, W)

    add(0, [y1], [f1])
    add(3, [f2, -a], [y1, f1])
    add(1, [y2, -f2, a], [f2, a, b])
    add(4, [f3 - h, u - w], [y1, f1])
    add(5, [f3, -(w + v), g + h, -u], [y2, f2, a, b])
    add(2, [y3, h - f3, w - u, -f3, w + v, -(g + h), u], [f3, w, g, v, h, u, q_])

    qc = pltpu.make_async_remote_copy(
        src_ref=phi.at[:, :, :, 1 - e], dst_ref=qrec,
        send_sem=q_s.at[0], recv_sem=q_r.at[0], device_id=(z, partner), device_id_type=MESH)
    qc.start()
    qc.wait_recv()
    qrec[...] += phi[:, :, :, e]
    s2a, s2a_mid, s2a_end = relay(
        lambda q, h: qrec.at[0:3, 2 * h:2 * h + 2, q], x2a, x2a_s, x2a_r, x, *xn)
    s2b, s2b_mid, s2b_end = relay(
        lambda q, h: qrec.at[3:6, q, 2 * h:2 * h + 2], x2b, x2b_s, x2b_r, y, *yn)
    s2a_mid()
    s2b_mid()
    r2a[:, 0:2], r2a[:, 2:4] = s2a_end()
    t2a = [exchange(r2a.at[:, (y + d) % 4], y2a, y2a_s, y2a_r, d, col_of((y + d) % 4, x)) for d in (2, 1, 3)]
    r2b[:, 0:2], r2b[:, 2:4] = s2b_end()
    t2b = [exchange(r2b.at[:, (x + d) % 4], y2b, y2b_s, y2b_r, d, col_of(y, (x + d) % 4)) for d in (2, 1, 3)]
    for cp in t2a:
        cp.wait_recv()
    sa = r2a[:, y] + y2a[0] + y2a[1] + y2a[2]
    for cp in t2b:
        cp.wait_recv()
    sb = r2b[:, x] + y2b[0] + y2b[1] + y2b[2]

    for zz in range(16):
        for i in range(6):
            src = sa[i] if i < 3 else sb[i - 3]
            zsend[zz, :, 16 * i:16 * i + 16] = src[:, 16 * zz:16 * zz + 16]
        zsend[zz, :, 96:128] = jnp.zeros((8, 32), F32)
    zc = []
    for d in (8, 7, 9, 6, 10, 5, 11, 4, 12, 3, 13, 2, 14, 1, 15):
        to = (z + d) % 16
        cp = pltpu.make_async_remote_copy(
            src_ref=zsend.at[to], dst_ref=zrec.at[d - 1], send_sem=z_s.at[d - 1], recv_sem=z_r.at[d - 1],
            device_id=(to, c), device_id_type=MESH)
        cp.start()
        zc.append(cp)
    for cp in zc:
        cp.wait_recv()
    tile = zsend[z]
    for d in range(15):
        tile = tile + zrec[d]
    ot[...] = tile

    for q in range(3):
        for s in range(8):
            ring_copy(z, s, q, up_s, up_r, up).wait_send()
        for s in range(7):
            ring_copy(z, s, q, dn_s, dn_r, down).wait_send()
    for i in range(16):
        @pl.when((i * 2 + half) != c)
        def _():
            for q in range(3):
                plane_copy(i, q).wait_send()
    near = [cp for _, cps in mid_of for cp in cps]
    for cp in pair + near + second[0] + second[1] + second[2] + second[3] + [qc] + s2a + s2b + t2a + t2b + zc:
        cp.wait_send()


def hand_out(blocks, tile, o1, o2, o3, ot):
    o1[...] = blocks[0]
    o2[...] = blocks[1]
    o3[...] = blocks[2]
    for i in range(6):
        ot[i] = tile[:, 16 * i:16 * i + 16]


def body(ancestor_inverse, panel_one, panel_two, panel_three, couplings, diag_terms, list_two, list_three):
    any_spec = pl.BlockSpec(memory_space=pl.ANY)
    vm = pl.BlockSpec(memory_space=pltpu.VMEM)
    dma = pltpu.SemaphoreType.DMA
    blocks, tile = pl.pallas_call(
        kernel,
        out_shape=(
            jax.ShapeDtypeStruct((3, ROWS, W), F32),
            jax.ShapeDtypeStruct((8, 128), F32),
        ),
        in_specs=[any_spec] * 6 + [vm] * 2,
        out_specs=(vm,) * 2,
        scratch_shapes=[
            pltpu.VMEM((1024, 512), F32),
            pltpu.VMEM((3, W, W), BF16),
            pltpu.VMEM((3, W, W), F32),
            pltpu.VMEM((16, 2, 32, 512), BF16),
            pltpu.VMEM((16, 2, 32, 512), BF16),
            pltpu.VMEM((16, 3, ROWS, W), BF16),
            pltpu.VMEM((3, 16, ROWS, W), BF16),
            pltpu.VMEM((4, 4, ROWS, 768), F32),
            pltpu.VMEM((4, 4, ROWS, 768), F32),
            pltpu.VMEM((4, 4, ROWS, 768), F32),
            *[pltpu.VMEM((6, 2, ROWS, hi - lo), F32) for lo, hi in STREAMS],
            *[pltpu.VMEM((3, ROWS, hi - lo), F32) for lo, hi in STREAMS],
            *[pltpu.VMEM((4, ROWS, hi - lo), F32) for lo, hi in STREAMS],
            pltpu.VMEM((ROWS, 768), F32),
            pltpu.VMEM((6, 4, 4, 2, 8, W), F32),
            pltpu.VMEM((6, 4, 4, 8, W), F32),
            pltpu.VMEM((6, 3, 2, 8, W), F32),
            pltpu.VMEM((3, 3, 8, W), F32),
            pltpu.VMEM((6, 3, 2, 8, W), F32),
            pltpu.VMEM((3, 3, 8, W), F32),
            pltpu.VMEM((3, 4, 8, W), F32),
            pltpu.VMEM((3, 4, 8, W), F32),
            pltpu.VMEM((16, 8, 128), F32),
            pltpu.VMEM((15, 8, 128), F32),
            dma((6,)), pltpu.SemaphoreType.REGULAR,
            dma((24,)), dma((24,)), dma((21,)), dma((21,)), dma((48,)), dma((48,)), dma((3,)), dma((3,)),
            dma((24,)), dma((24,)), dma((12,)), dma((12,)),
            dma((1,)), dma((1,)), dma((6,)), dma((6,)), dma((3,)), dma((3,)), dma((6,)), dma((6,)),
            dma((3,)), dma((3,)), dma((15,)), dma((15,)),
        ],
        compiler_params=pltpu.CompilerParams(
            collective_id=0, has_side_effects=True, vmem_limit_bytes=56 << 20
        ),
        name="chain_inverse",
    )(
        ancestor_inverse, panel_one, panel_two, panel_three, couplings, diag_terms,
        list_two.reshape(1, -1), list_three.reshape(1, -1),
    )
    *inverses, small = pl.pallas_call(
        hand_out,
        out_shape=(jax.ShapeDtypeStruct((ROWS, W), F32),) * 3 + (jax.ShapeDtypeStruct((6, 8, 16), F32),),
        in_specs=[vm] * 2,
        out_specs=(vm,) * 4,
        name="hand_out",
    )(blocks, tile)
    return (*inverses, jnp.swapaxes(small, 1, 2))


def solution(mesh):
    rows = P(("row", "col"), None)
    return jax.shard_map(
        body,
        mesh=mesh,
        in_specs=(P("row", "col"), rows, rows, rows, P(), P(), P(), P()),
        out_specs=(rows, rows, rows, P(None, "row", "col")),
        check_vma=False,
    )
```

time: 91 us -> 87.6 us (0.963)
  Pallas kernels: 89.3 us -> 86.7 us
    pallas_call x1, Pallas kernels: 87.7 us -> 85.2 us  [body(): pl.pallas_call(kernel, out_shape=(jax.ShapeDtypeStruct((3, ROWS, W), F32)...]
where the time goes in v3:
time: 87.6 us; the launch traced here: 87.4 us
  Pallas kernels  86.7 us (99%)
    pallas_call x1, Pallas kernels, body(): pl.pallas_call(kernel, out_shape=(jax.ShapeDtypeStruct((3, ROWS, W), F32)...  85.2 us

profile of v3, /device:TPU:1, one launch (start us, length us, event | category | flops | bytes accessed | tf_op | source)
XLA Modules:
  0.0 87.4 jit_solution(367290933916344799)
XLA Ops:
  0.6 85.2 %chain_inverse.1 = (f32[3,32,256]{2,1,0:T(8,128)}, f32[8,128]{1,0:T(8,128)}) custom-call(f32[1024,512]{1,0:T(8,128)} %a_hbm.1, bf16[32,256]{1,0:T(8,128)(2,1)} %p1.1, bf16[32,256]{1,0:T(8,128)(2,1)} %p2.1, bf16[32,256]{1,0:T(8,128)(2,1)} %p3.1, bf16[3,256,256]{2,1,0:T(8,128)(2,1)} %coup_hbm.1, f32[3,256,256]{2,1,0:T(8,128)} %diag_hbm.1, s32[1,60]{1,0:T(1,128)} %bitcast.3, ...), custom_call_target="tpu_custom_call" | custom-call | tf_op jit(solution)/shard_map/chain_inverse/pallas_call | solution.py:394
  85.8 1.6 %hand_out.1 = (f32[32,256]{1,0:T(8,128)}, f32[32,256]{1,0:T(8,128)}, f32[32,256]{1,0:T(8,128)}, f32[6,8,16]{2,1,0:T(8,128)}) custom-call(f32[3,32,256]{2,1,0:T(8,128)} %get-tuple-element.10.blocks, f32[8,128]{1,0:T(8,128)} %get-tuple-element.11.tile), custom_call_target="tpu_custom_call" | custom-call | tf_op jit(solution)/shard_map/hand_out/pallas_call | solution.py:441

commit v4 on v3

--- a/solution.py
+++ b/solution.py
@@ -11,6 +11,8 @@
 F32 = jnp.float32
 BF16 = jnp.bfloat16
 NZ, NK, W, ROWS = 16, 16, 256, 32
+REACH = {1: 8, -1: 7}
+GROUPS = ((0, 0, 256, True), (3, 0, 128, True), (3, 128, 256, False))
 STREAMS = ((0, 256), (256, 512), (512, 640), (640, 768))
 
 
@@ -53,10 +55,10 @@
     o, ot,
     a_vm, coup, diag, ahi, alo, ring, fbuf, pown, ppar, prec,
     rec0, rec1, rec2, rec3, far0, far1, far2, far3, mid0, mid1, mid2, mid3, ysum,
-    phi, qrec, x2a, y2a, x2b, y2b, r2a, r2b, zsend, zrec,
+    phi, qrec, ga_rec, gb_rec, gc_rec, ga_far, gb_far, gc_far, ga_mid, gb_mid, gc_mid, zsend, zrec,
     lsem, in_sem, up_s, up_r, dn_s, dn_r, f_s, f_r, pr_s, pr_r,
     rel_s, rel_r, far_s, far_r,
-    q_s, q_r, x2a_s, x2a_r, y2a_s, y2a_r, x2b_s, x2b_r, y2b_s, y2b_r, z_s, z_r,
+    q_s, q_r, g_s, g_r, gf_s, gf_r, z_s, z_r,
 ):
     z = lax.axis_index("row")
     c = lax.axis_index("col")
@@ -90,22 +92,34 @@
             cross.append(((y + d) % 4 * 4 + x) * 2 + ee)
     for to in line + cross:
         pl.semaphore_signal(barrier, inc=1, device_id=(z, to), device_id_type=MESH)
-    for d in (1, 15):
+    for d in (1, 2, 14, 15):
         pl.semaphore_signal(barrier, inc=1, device_id=((z + d) % 16, c), device_id_type=MESH)
     for cp in own:
         cp.wait()
-    pl.semaphore_wait(barrier, 15)
+    pl.semaphore_wait(barrier, 17)
     for to in cross:
         pl.semaphore_signal(in_sem, inc=1, device_id=(z, to), device_id_type=MESH)
 
-    up, down = (z + 1) % 16, (z + 15) % 16
     slot = (k % 8) * 2 + e
 
-    def ring_copy(item, s, q, send, recv, to):
+    def hop(item, dist, step, q, way):
+        send, recv = (up_s, up_r) if way > 0 else (dn_s, dn_r)
         part = ring.at[item, q]
+        n = 3 * (dist + step - 1) + q
         return pltpu.make_async_remote_copy(
-            src_ref=part, dst_ref=part, send_sem=send.at[3 * s + q], recv_sem=recv.at[3 * s + q],
-            device_id=(to, c), device_id_type=MESH)
+            src_ref=part, dst_ref=part, send_sem=send.at[n], recv_sem=recv.at[n],
+            device_id=((z + 16 + way * step) % 16, c), device_id_type=MESH)
+
+    def item_at(dist, way):
+        return (z + 16 - way * dist) % 16
+
+    def push(dist, q, way):
+        for step in (2, 1):
+            if dist + step <= REACH[way]:
+                hop(item_at(dist, way), dist, step, q, way).start()
+
+    def landed(dist, q, way):
+        hop(item_at(dist, way), dist - 1, 1, q, way).wait_recv()
 
     def plane_copy(item, q):
         return pltpu.make_async_remote_copy(
@@ -125,23 +139,20 @@
             plane_copy(item, q).start()
 
     for q in range(3):
-        ring_copy(z, 0, q, up_s, up_r, up).start()
-        ring_copy(z, 0, q, dn_s, dn_r, down).start()
+        for way in (1, -1):
+            push(0, q, way)
     pl.semaphore_wait(in_sem, 6)
     for q in range(3):
         spread(z, q)
-    for s in range(1, 9):
-        below, above = (z + 16 - s) % 16, (z + s) % 16
-        for q in range(3):
-            ring_copy(below, s - 1, q, up_s, up_r, up).wait_recv()
-            if s < 8:
-                ring_copy(below, s, q, up_s, up_r, up).start()
-                ring_copy(above, s - 1, q, dn_s, dn_r, down).wait_recv()
-            if s < 7:
-                ring_copy(above, s, q, dn_s, dn_r, down).start()
-            spread(below, q)
-            if s < 8:
-                spread(above, q)
+    for dist in (2, 4, 6, 8):
+        for at in (dist, dist - 1):
+            for q in range(3):
+                for way in (1, -1):
+                    if at <= REACH[way]:
+                        landed(at, q, way)
+                        if at == dist:
+                            push(at, q, way)
+                        spread(item_at(at, way), q)
 
     lines2 = l2[...]
     lines3 = l3[...]
@@ -290,65 +301,106 @@
     h31 = -(mm(g1, c1) + mm(h21, c2))
     h32 = -(tmc(h21, c1) + mm(g2, c2))
     g3 = diag[2] - ctm(c1, h31) - ctm(c2, h32)
-    for i, v in enumerate((g1, g2, g3, h21, h31, h32)):
+    for i, v in enumerate((g1, h21, h31, g2, h32, g3)):
         phi[i] = (v.T * first).reshape(4, 4, 2, 8, W)
 
     second_stage(1)
     second_stage(2)
     second_stage(3)
-    for n in range(4):
-        close_stream(n)
-
+    def add(i, right, left):
+        val = tmm(jnp.concatenate(right, axis=0), jnp.concatenate(left, axis=0))
+        phi[i] += val.reshape(4, 4, 2, 8, W)
+
+    def pair_terms(n):
+        three = slice(3 * n, 3 * n + 3)
+        cp = pltpu.make_async_remote_copy(
+            src_ref=phi.at[three, :, :, 1 - e], dst_ref=qrec.at[three],
+            send_sem=q_s.at[n], recv_sem=q_r.at[n], device_id=(z, partner), device_id_type=MESH)
+        cp.start()
+        return cp
+
+    group_far = (ga_far, gb_far, gc_far)
+    group_mid = (ga_mid, gb_mid, gc_mid)
+    group_rec = (ga_rec, gb_rec, gc_rec)
+    groups = {}
+
+    def open_group(n):
+        blk, lo, hi, xfirst = GROUPS[n]
+        three = slice(blk, blk + 3)
+        if xfirst:
+            r = relay(lambda q, h: qrec.at[three, 2 * h:2 * h + 2, q, :, lo:hi],
+                      group_rec[n], g_s, g_r, x, *xn, base=6 * n)
+        else:
+            r = relay(lambda q, h: qrec.at[three, q, 2 * h:2 * h + 2, :, lo:hi],
+                      group_rec[n], g_s, g_r, y, *yn, base=6 * n)
+        groups[n] = r
+
+    def second_group(n):
+        xfirst = GROUPS[n][3]
+        group_mid[n][:, 0:2], group_mid[n][:, 2:4] = groups[n][2]()
+        cps = []
+        for d in (2, 1, 3):
+            if xfirst:
+                src, to = group_mid[n].at[:, (y + d) % 4], col_of((y + d) % 4, x)
+            else:
+                src, to = group_mid[n].at[:, (x + d) % 4], col_of(y, (x + d) % 4)
+            cps.append(exchange(src, group_far[n], gf_s, gf_r, d, to, n=3 * n))
+        return cps
+
+    def close_group(n, cps):
+        for cp in cps:
+            cp.wait_recv()
+        far = group_far[n]
+        return group_mid[n][:, y if GROUPS[n][3] else x] + far[0] + far[1] + far[2]
+
+    def pack(blk, val):
+        for zz in range(16):
+            for i in range(3):
+                at = 16 * (blk + i)
+                zsend[zz, :, at:at + 16] = val[i][:, 16 * zz:16 * zz + 16]
+
+    close_stream(0)
     y1 = ysum[:, 0:W]
     a = mm(y1, c0)
     w = mm(y1, c1)
+    u = mm(a, c2)
+    add(0, [y1], [f1])
+    add(1, [f2, -a], [y1, f1])
+    add(2, [f3 - h, u - w], [y1, f1])
+    terms = [pair_terms(0)]
+    o[0] = -y1
+    close_stream(1)
     y2 = (ysum[:, W:2 * W] - a) * keep2
+    o[1] = -y2
     v = mm(y2, c2)
-    u = mm(a, c2)
+    add(3, [y2, -f2, a], [f2, a, b])
+    add(4, [f3, -(w + v), g + h, -u], [y2, f2, a, b])
+    close_stream(2)
+    close_stream(3)
+    terms[0].wait_recv()
+    qrec[0:3] += phi[0:3, :, :, e]
+    open_group(0)
     y3 = (ysum[:, 2 * W:3 * W] - w - v) * keep3
-    o[0] = -y1
-    o[1] = -y2
+    add(5, [y3, h - f3, w - u, -f3, w + v, -(g + h), u], [f3, w, g, v, h, u, q_])
+    terms.append(pair_terms(1))
     o[2] = -y3
-
-    def add(i, right, left):
-        val = tmm(jnp.concatenate(right, axis=0), jnp.concatenate(left, axis=0))
-        phi[i] += val.reshape(4, 4, 2, 8, W)
-
-    add(0, [y1], [f1])
-    add(3, [f2, -a], [y1, f1])
-    add(1, [y2, -f2, a], [f2, a, b])
-    add(4, [f3 - h, u - w], [y1, f1])
-    add(5, [f3, -(w + v), g + h, -u], [y2, f2, a, b])
-    add(2, [y3, h - f3, w - u, -f3, w + v, -(g + h), u], [f3, w, g, v, h, u, q_])
-
-    qc = pltpu.make_async_remote_copy(
-        src_ref=phi.at[:, :, :, 1 - e], dst_ref=qrec,
-        send_sem=q_s.at[0], recv_sem=q_r.at[0], device_id=(z, partner), device_id_type=MESH)
-    qc.start()
-    qc.wait_recv()
-    qrec[...] += phi[:, :, :, e]
-    s2a, s2a_mid, s2a_end = relay(
-        lambda q, h: qrec.at[0:3, 2 * h:2 * h + 2, q], x2a, x2a_s, x2a_r, x, *xn)
-    s2b, s2b_mid, s2b_end = relay(
-        lambda q, h: qrec.at[3:6, q, 2 * h:2 * h + 2], x2b, x2b_s, x2b_r, y, *yn)
-    s2a_mid()
-    s2b_mid()
-    r2a[:, 0:2], r2a[:, 2:4] = s2a_end()
-    t2a = [exchange(r2a.at[:, (y + d) % 4], y2a, y2a_s, y2a_r, d, col_of((y + d) % 4, x)) for d in (2, 1, 3)]
-    r2b[:, 0:2], r2b[:, 2:4] = s2b_end()
-    t2b = [exchange(r2b.at[:, (x + d) % 4], y2b, y2b_s, y2b_r, d, col_of(y, (x + d) % 4)) for d in (2, 1, 3)]
-    for cp in t2a:
-        cp.wait_recv()
-    sa = r2a[:, y] + y2a[0] + y2a[1] + y2a[2]
-    for cp in t2b:
-        cp.wait_recv()
-    sb = r2b[:, x] + y2b[0] + y2b[1] + y2b[2]
-
+    groups[0][1]()
+    terms[1].wait_recv()
+    qrec[3:6] += phi[3:6, :, :, e]
+    open_group(1)
+    open_group(2)
+    last = [second_group(0)]
+    groups[1][1]()
+    groups[2][1]()
     for zz in range(16):
-        for i in range(6):
-            src = sa[i] if i < 3 else sb[i - 3]
-            zsend[zz, :, 16 * i:16 * i + 16] = src[:, 16 * zz:16 * zz + 16]
         zsend[zz, :, 96:128] = jnp.zeros((8, 32), F32)
+    pack(0, close_group(0, last[0]))
+    last.append(second_group(1))
+    last.append(second_group(2))
+    left = close_group(1, last[1])
+    right = close_group(2, last[2])
+    pack(3, jnp.concatenate([left, right], axis=2))
+
     zc = []
     for d in (8, 7, 9, 6, 10, 5, 11, 4, 12, 3, 13, 2, 14, 1, 15):
         to = (z + d) % 16
@@ -364,18 +416,18 @@
         tile = tile + zrec[d]
     ot[...] = tile
 
-    for q in range(3):
-        for s in range(8):
-            ring_copy(z, s, q, up_s, up_r, up).wait_send()
-        for s in range(7):
-            ring_copy(z, s, q, dn_s, dn_r, down).wait_send()
+    for way in (1, -1):
+        for dist in range(1, REACH[way] + 1):
+            for q in range(3):
+                hop(z, dist - 1, 1, q, way).wait_send()
     for i in range(16):
         @pl.when((i * 2 + half) != c)
         def _():
             for q in range(3):
                 plane_copy(i, q).wait_send()
     near = [cp for _, cps in mid_of for cp in cps]
-    for cp in pair + near + second[0] + second[1] + second[2] + second[3] + [qc] + s2a + s2b + t2a + t2b + zc:
+    near += [cp for n in range(3) for cp in groups[n][0] + last[n]]
+    for cp in pair + near + second[0] + second[1] + second[2] + second[3] + terms + zc:
         cp.wait_send()
 
 
@@ -383,8 +435,8 @@
     o1[...] = blocks[0]
     o2[...] = blocks[1]
     o3[...] = blocks[2]
-    for i in range(6):
-        ot[i] = tile[:, 16 * i:16 * i + 16]
+    for i, n in enumerate((0, 3, 5, 1, 2, 4)):
+        ot[i] = tile[:, 16 * n:16 * n + 16]
 
 
 def body(ancestor_inverse, panel_one, panel_two, panel_three, couplings, diag_terms, list_two, list_three):
@@ -416,19 +468,15 @@
             pltpu.VMEM((ROWS, 768), F32),
             pltpu.VMEM((6, 4, 4, 2, 8, W), F32),
             pltpu.VMEM((6, 4, 4, 8, W), F32),
-            pltpu.VMEM((6, 3, 2, 8, W), F32),
-            pltpu.VMEM((3, 3, 8, W), F32),
-            pltpu.VMEM((6, 3, 2, 8, W), F32),
-            pltpu.VMEM((3, 3, 8, W), F32),
-            pltpu.VMEM((3, 4, 8, W), F32),
-            pltpu.VMEM((3, 4, 8, W), F32),
+            *[pltpu.VMEM((6, 3, 2, 8, hi - lo), F32) for _, lo, hi, _ in GROUPS],
+            *[pltpu.VMEM((3, 3, 8, hi - lo), F32) for _, lo, hi, _ in GROUPS],
+            *[pltpu.VMEM((3, 4, 8, hi - lo), F32) for _, lo, hi, _ in GROUPS],
             pltpu.VMEM((16, 8, 128), F32),
             pltpu.VMEM((15, 8, 128), F32),
             dma((6,)), pltpu.SemaphoreType.REGULAR,
             dma((24,)), dma((24,)), dma((21,)), dma((21,)), dma((48,)), dma((48,)), dma((3,)), dma((3,)),
             dma((24,)), dma((24,)), dma((12,)), dma((12,)),
-            dma((1,)), dma((1,)), dma((6,)), dma((6,)), dma((3,)), dma((3,)), dma((6,)), dma((6,)),
-            dma((3,)), dma((3,)), dma((15,)), dma((15,)),
+            dma((2,)), dma((2,)), dma((18,)), dma((18,)), dma((9,)), dma((9,)), dma((15,)), dma((15,)),
         ],
         compiler_params=pltpu.CompilerParams(
             collective_id=0, has_side_effects=True, vmem_limit_bytes=56 << 20

time: 87.6 us -> 84.7 us (0.967)
  the two profiles are of different devices: /device:TPU:1 before, /device:TPU:2 now
where the time goes in v4:
time: 84.7 us; the launch traced here: 84.5 us
  Pallas kernels  83.8 us (99%)
    pallas_call x1, Pallas kernels, body(): pl.pallas_call(kernel, out_shape=(jax.ShapeDtypeStruct((3, ROWS, W), F32)...  82.3 us

profile of v4, /device:TPU:2, one launch (start us, length us, event | category | flops | bytes accessed | tf_op | source)
XLA Modules:
  0.0 84.5 jit_solution(325445963463128963)
XLA Ops:
  0.6 82.3 %chain_inverse.1 = (f32[3,32,256]{2,1,0:T(8,128)}, f32[8,128]{1,0:T(8,128)}) custom-call(f32[1024,512]{1,0:T(8,128)} %a_hbm.1, bf16[32,256]{1,0:T(8,128)(2,1)} %p1.1, bf16[32,256]{1,0:T(8,128)(2,1)} %p2.1, bf16[32,256]{1,0:T(8,128)(2,1)} %p3.1, bf16[3,256,256]{2,1,0:T(8,128)(2,1)} %coup_hbm.1, f32[3,256,256]{2,1,0:T(8,128)} %diag_hbm.1, s32[1,60]{1,0:T(1,128)} %bitcast.3, ...), custom_call_target="tpu_custom_call" | custom-call | tf_op jit(solution)/shard_map/chain_inverse/pallas_call | solution.py:446
  82.9 1.6 %hand_out.1 = (f32[32,256]{1,0:T(8,128)}, f32[32,256]{1,0:T(8,128)}, f32[32,256]{1,0:T(8,128)}, f32[6,8,16]{2,1,0:T(8,128)}) custom-call(f32[3,32,256]{2,1,0:T(8,128)} %get-tuple-element.10.blocks, f32[8,128]{1,0:T(8,128)} %get-tuple-element.11.tile), custom_call_target="tpu_custom_call" | custom-call | tf_op jit(solution)/shard_map/hand_out/pallas_call | solution.py:489

commit v5 on v4

--- a/solution.py
+++ b/solution.py
@@ -12,7 +12,10 @@
 BF16 = jnp.bfloat16
 NZ, NK, W, ROWS = 16, 16, 256, 32
 REACH = {1: 8, -1: 7}
-GROUPS = ((0, 0, 256, True), (3, 0, 128, True), (3, 128, 256, False))
+GROUPS = (
+    (0, 3, 0, 256, True), (3, 2, 0, 128, True), (3, 2, 128, 256, False), (5, 1, 0, 128, True), (5, 1, 128, 256, False),
+)
+SETS = ((0, 3), (3, 2), (5, 1))
 STREAMS = ((0, 256), (256, 512), (512, 640), (640, 768))
 
 
@@ -55,7 +58,7 @@
     o, ot,
     a_vm, coup, diag, ahi, alo, ring, fbuf, pown, ppar, prec,
     rec0, rec1, rec2, rec3, far0, far1, far2, far3, mid0, mid1, mid2, mid3, ysum,
-    phi, qrec, ga_rec, gb_rec, gc_rec, ga_far, gb_far, gc_far, ga_mid, gb_mid, gc_mid, zsend, zrec,
+    phi, qrec, zsend, zrec, gr,
     lsem, in_sem, up_s, up_r, dn_s, dn_r, f_s, f_r, pr_s, pr_r,
     rel_s, rel_r, far_s, far_r,
     q_s, q_r, g_s, g_r, gf_s, gf_r, z_s, z_r,
@@ -144,7 +147,7 @@
     pl.semaphore_wait(in_sem, 6)
     for q in range(3):
         spread(z, q)
-    for dist in (2, 4, 6, 8):
+    def level(dist):
         for at in (dist, dist - 1):
             for q in range(3):
                 for way in (1, -1):
@@ -159,6 +162,7 @@
     block = (z * 32 + c) // 8
     keep2 = keep_of(lines2, block)
     keep3 = keep_of(lines3, block)
+    level(2)
     acopy.wait()
 
     @pl.loop(0, 16)
@@ -167,9 +171,20 @@
         ahi[i] = hi.reshape(2, 32, 512)
         alo[i] = lo.reshape(2, 32, 512)
 
+    level(4)
     ccopy.wait()
     dcopy.wait()
     c0, c1, c2 = coup[0], coup[1], coup[2]
+    first = jnp.where((z == 0) & (c == 0), 1.0, 0.0).astype(F32)
+    g1 = diag[0]
+    h21 = -mm(g1, c0)
+    g2 = diag[1] - ctm(c0, h21)
+    level(6)
+    h31 = -(mm(g1, c1) + mm(h21, c2))
+    h32 = -(tmc(h21, c1) + mm(g2, c2))
+    g3 = diag[2] - ctm(c1, h31) - ctm(c2, h32)
+    for i, v in enumerate((g1, h21, h31, g2, h32, g3)):
+        phi[i] = (v.T * first).reshape(4, 4, 2, 8, W)
     f1 = ring[z, 0].astype(F32)
     f2 = ring[z, 1].astype(F32) * keep2
     f3 = ring[z, 2].astype(F32) * keep3
@@ -177,6 +192,7 @@
     g = mm(f1, c1)
     h = mm(f2, c2)
     q_ = mm(b, c2)
+    level(8)
 
     def arrived(q):
         for i in range(16):
@@ -293,17 +309,6 @@
     second_stage(0)
     mid_of[2][0]()
     mid_of[3][0]()
-
-    first = jnp.where((z == 0) & (c == 0), 1.0, 0.0).astype(F32)
-    g1 = diag[0]
-    h21 = -mm(g1, c0)
-    g2 = diag[1] - ctm(c0, h21)
-    h31 = -(mm(g1, c1) + mm(h21, c2))
-    h32 = -(tmc(h21, c1) + mm(g2, c2))
-    g3 = diag[2] - ctm(c1, h31) - ctm(c2, h32)
-    for i, v in enumerate((g1, h21, h31, g2, h32, g3)):
-        phi[i] = (v.T * first).reshape(4, 4, 2, 8, W)
-
     second_stage(1)
     second_stage(2)
     second_stage(3)
@@ -312,53 +317,61 @@
         phi[i] += val.reshape(4, 4, 2, 8, W)
 
     def pair_terms(n):
-        three = slice(3 * n, 3 * n + 3)
+        at = pl.ds(*SETS[n])
         cp = pltpu.make_async_remote_copy(
-            src_ref=phi.at[three, :, :, 1 - e], dst_ref=qrec.at[three],
+            src_ref=phi.at[at, :, :, 1 - e], dst_ref=qrec.at[at],
             send_sem=q_s.at[n], recv_sem=q_r.at[n], device_id=(z, partner), device_id_type=MESH)
         cp.start()
         return cp
 
-    group_far = (ga_far, gb_far, gc_far)
-    group_mid = (ga_mid, gb_mid, gc_mid)
-    group_rec = (ga_rec, gb_rec, gc_rec)
-    groups = {}
-
-    def open_group(n):
-        blk, lo, hi, xfirst = GROUPS[n]
-        three = slice(blk, blk + 3)
-        if xfirst:
-            r = relay(lambda q, h: qrec.at[three, 2 * h:2 * h + 2, q, :, lo:hi],
-                      group_rec[n], g_s, g_r, x, *xn, base=6 * n)
-        else:
-            r = relay(lambda q, h: qrec.at[three, q, 2 * h:2 * h + 2, :, lo:hi],
-                      group_rec[n], g_s, g_r, y, *yn, base=6 * n)
-        groups[n] = r
+    group_rec, group_far, group_mid = gr[0::3], gr[1::3], gr[2::3]
+    ga_rec, ga_mid = group_rec[0], group_mid[0]
+
+    def met(n):
+        terms[n].wait_recv()
+        at = slice(SETS[n][0], SETS[n][0] + SETS[n][1])
+        qrec[at] += phi[at, :, :, e]
+
+    def spots(n, first_stage):
+        along_x = GROUPS[n][4] == first_stage
+        out = [((x + d) % 4, col_of(y, (x + d) % 4)) if along_x else ((y + d) % 4, col_of((y + d) % 4, x))
+               for d in range(4)]
+        return out
+
+    def slab(n, q):
+        blk, nb, lo, hi, xfirst = GROUPS[n]
+        at = pl.ds(blk, nb)
+        return qrec.at[at, :, q, :, lo:hi] if xfirst else qrec.at[at, q, :, :, lo:hi]
+
+    def open_direct(n):
+        to = spots(n, True)
+        return [exchange(slab(n, to[d][0]), group_rec[n], g_s, g_r, d, to[d][1], n=3 + 3 * n) for d in (2, 1, 3)]
 
     def second_group(n):
-        xfirst = GROUPS[n][3]
-        group_mid[n][:, 0:2], group_mid[n][:, 2:4] = groups[n][2]()
-        cps = []
-        for d in (2, 1, 3):
-            if xfirst:
-                src, to = group_mid[n].at[:, (y + d) % 4], col_of((y + d) % 4, x)
-            else:
-                src, to = group_mid[n].at[:, (x + d) % 4], col_of(y, (x + d) % 4)
-            cps.append(exchange(src, group_far[n], gf_s, gf_r, d, to, n=3 * n))
-        return cps
+        to = spots(n, False)
+        return [exchange(group_mid[n].at[:, to[d][0]], group_far[n], gf_s, gf_r, d, to[d][1], n=3 * n)
+                for d in (2, 1, 3)]
+
+    def turn_direct(n, cps):
+        for cp in cps:
+            cp.wait_recv()
+        rec = group_rec[n]
+        group_mid[n][...] = slab(n, x if GROUPS[n][4] else y)[...] + rec[0] + rec[1] + rec[2]
+        return second_group(n)
 
     def close_group(n, cps):
         for cp in cps:
             cp.wait_recv()
         far = group_far[n]
-        return group_mid[n][:, y if GROUPS[n][3] else x] + far[0] + far[1] + far[2]
+        return group_mid[n][:, y if GROUPS[n][4] else x] + far[0] + far[1] + far[2]
 
     def pack(blk, val):
         for zz in range(16):
-            for i in range(3):
+            for i in range(val.shape[0]):
                 at = 16 * (blk + i)
                 zsend[zz, :, at:at + 16] = val[i][:, 16 * zz:16 * zz + 16]
 
+    terms = []
     close_stream(0)
     y1 = ysum[:, 0:W]
     a = mm(y1, c0)
@@ -367,39 +380,42 @@
     add(0, [y1], [f1])
     add(1, [f2, -a], [y1, f1])
     add(2, [f3 - h, u - w], [y1, f1])
-    terms = [pair_terms(0)]
+    terms.append(pair_terms(0))
     o[0] = -y1
     close_stream(1)
     y2 = (ysum[:, W:2 * W] - a) * keep2
-    o[1] = -y2
     v = mm(y2, c2)
     add(3, [y2, -f2, a], [f2, a, b])
     add(4, [f3, -(w + v), g + h, -u], [y2, f2, a, b])
+    terms.append(pair_terms(1))
+    o[1] = -y2
+    met(0)
+    wide, wide_mid, wide_end = relay(
+        lambda q, hh: qrec.at[0:3, 2 * hh:2 * hh + 2, q], ga_rec, g_s, g_r, x, *xn)
+    for zz in range(16):
+        zsend[zz, :, 96:128] = jnp.zeros((8, 32), F32)
     close_stream(2)
     close_stream(3)
-    terms[0].wait_recv()
-    qrec[0:3] += phi[0:3, :, :, e]
-    open_group(0)
     y3 = (ysum[:, 2 * W:3 * W] - w - v) * keep3
     add(5, [y3, h - f3, w - u, -f3, w + v, -(g + h), u], [f3, w, g, v, h, u, q_])
-    terms.append(pair_terms(1))
+    terms.append(pair_terms(2))
     o[2] = -y3
-    groups[0][1]()
-    terms[1].wait_recv()
-    qrec[3:6] += phi[3:6, :, :, e]
-    open_group(1)
-    open_group(2)
-    last = [second_group(0)]
-    groups[1][1]()
-    groups[2][1]()
-    for zz in range(16):
-        zsend[zz, :, 96:128] = jnp.zeros((8, 32), F32)
-    pack(0, close_group(0, last[0]))
-    last.append(second_group(1))
-    last.append(second_group(2))
-    left = close_group(1, last[1])
-    right = close_group(2, last[2])
-    pack(3, jnp.concatenate([left, right], axis=2))
+    met(1)
+    firsts, lasts = {}, {}
+    for n in (1, 2):
+        firsts[n] = open_direct(n)
+    wide_mid()
+    met(2)
+    for n in (3, 4):
+        firsts[n] = open_direct(n)
+    ga_mid[:, 0:2], ga_mid[:, 2:4] = wide_end()
+    lasts[0] = second_group(0)
+    for n in (1, 2, 3, 4):
+        lasts[n] = turn_direct(n, firsts[n])
+    pack(0, close_group(0, lasts[0]))
+    for n, blk in ((1, 3), (3, 5)):
+        left, right = close_group(n, lasts[n]), close_group(n + 1, lasts[n + 1])
+        pack(blk, jnp.concatenate([left, right], axis=2))
 
     zc = []
     for d in (8, 7, 9, 6, 10, 5, 11, 4, 12, 3, 13, 2, 14, 1, 15):
@@ -426,7 +442,7 @@
             for q in range(3):
                 plane_copy(i, q).wait_send()
     near = [cp for _, cps in mid_of for cp in cps]
-    near += [cp for n in range(3) for cp in groups[n][0] + last[n]]
+    near += wide + [cp for n in firsts for cp in firsts[n]] + [cp for n in lasts for cp in lasts[n]]
     for cp in pair + near + second[0] + second[1] + second[2] + second[3] + terms + zc:
         cp.wait_send()
 
@@ -468,15 +484,14 @@
             pltpu.VMEM((ROWS, 768), F32),
             pltpu.VMEM((6, 4, 4, 2, 8, W), F32),
             pltpu.VMEM((6, 4, 4, 8, W), F32),
-            *[pltpu.VMEM((6, 3, 2, 8, hi - lo), F32) for _, lo, hi, _ in GROUPS],
-            *[pltpu.VMEM((3, 3, 8, hi - lo), F32) for _, lo, hi, _ in GROUPS],
-            *[pltpu.VMEM((3, 4, 8, hi - lo), F32) for _, lo, hi, _ in GROUPS],
             pltpu.VMEM((16, 8, 128), F32),
             pltpu.VMEM((15, 8, 128), F32),
+            [pltpu.VMEM(shape, F32) for n, (_, nb, lo, hi, _) in enumerate(GROUPS) for shape in (
+                (3, nb, 4, 8, hi - lo) if n else (6, nb, 2, 8, hi - lo), (3, nb, 8, hi - lo), (nb, 4, 8, hi - lo))],
             dma((6,)), pltpu.SemaphoreType.REGULAR,
             dma((24,)), dma((24,)), dma((21,)), dma((21,)), dma((48,)), dma((48,)), dma((3,)), dma((3,)),
             dma((24,)), dma((24,)), dma((12,)), dma((12,)),
-            dma((2,)), dma((2,)), dma((18,)), dma((18,)), dma((9,)), dma((9,)), dma((15,)), dma((15,)),
+            dma((3,)), dma((3,)), dma((18,)), dma((18,)), dma((15,)), dma((15,)), dma((15,)), dma((15,)),
         ],
         compiler_params=pltpu.CompilerParams(
             collective_id=0, has_side_effects=True, vmem_limit_bytes=56 << 20

time: 84.7 us -> 79.6 us (0.940)
  the two profiles are of different devices: /device:TPU:2 before, /device:TPU:1 now
where the time goes in v5:
time: 79.6 us; the launch traced here: 79.4 us
  Pallas kernels  78.8 us (99%)
    pallas_call x1, Pallas kernels, body(): pl.pallas_call(kernel, out_shape=(jax.ShapeDtypeStruct((3, ROWS, W), F32)...  77.2 us

profile of v5, /device:TPU:1, one launch (start us, length us, event | category | flops | bytes accessed | tf_op | source)
XLA Modules:
  0.0 79.4 jit_solution(6233862463589225241)
XLA Ops:
  0.6 77.2 %chain_inverse.1 = (f32[3,32,256]{2,1,0:T(8,128)}, f32[8,128]{1,0:T(8,128)}) custom-call(f32[1024,512]{1,0:T(8,128)} %a_hbm.1, bf16[32,256]{1,0:T(8,128)(2,1)} %p1.1, bf16[32,256]{1,0:T(8,128)(2,1)} %p2.1, bf16[32,256]{1,0:T(8,128)(2,1)} %p3.1, bf16[3,256,256]{2,1,0:T(8,128)(2,1)} %coup_hbm.1, f32[3,256,256]{2,1,0:T(8,128)} %diag_hbm.1, s32[1,60]{1,0:T(1,128)} %bitcast.3, ...), custom_call_target="tpu_custom_call" | custom-call | tf_op jit(solution)/shard_map/chain_inverse/pallas_call | solution.py:462
  77.8 1.6 %hand_out.1 = (f32[32,256]{1,0:T(8,128)}, f32[32,256]{1,0:T(8,128)}, f32[32,256]{1,0:T(8,128)}, f32[6,8,16]{2,1,0:T(8,128)}) custom-call(f32[3,32,256]{2,1,0:T(8,128)} %get-tuple-element.10.blocks, f32[8,128]{1,0:T(8,128)} %get-tuple-element.11.tile), custom_call_target="tpu_custom_call" | custom-call | tf_op jit(solution)/shard_map/hand_out/pallas_call | solution.py:504

commit v6 on v5

--- a/solution.py
+++ b/solution.py
@@ -184,7 +184,8 @@
     h32 = -(tmc(h21, c1) + mm(g2, c2))
     g3 = diag[2] - ctm(c1, h31) - ctm(c2, h32)
     for i, v in enumerate((g1, h21, h31, g2, h32, g3)):
-        phi[i] = (v.T * first).reshape(4, 4, 2, 8, W)
+        for side in range(2):
+            phi[i, side] = (v.T * first).reshape(4, 4, 2, 8, W)[:, :, side]
     f1 = ring[z, 0].astype(F32)
     f2 = ring[z, 1].astype(F32) * keep2
     f3 = ring[z, 2].astype(F32) * keep3
@@ -209,22 +210,25 @@
         out = out + jnp.dot(alo[:, side].reshape(512, 512), f, preferred_element_type=F32)
         return out.reshape(4, 4, ROWS, W)
 
-    def panel(q):
-        return pl.ds(q * W, W)
+    def put(bufs, q, val):
+        for n, (lo, hi) in enumerate(STREAMS):
+            if q * W <= lo < (q + 1) * W:
+                bufs[n][...] = val[:, :, :, lo - q * W:hi - q * W]
 
     pair = []
 
     def to_partner(q):
-        ppar[:, :, :, panel(q)] = part(1 - e, q)
-        cp = pltpu.make_async_remote_copy(
-            src_ref=ppar.at[:, :, :, panel(q)], dst_ref=prec.at[:, :, :, panel(q)],
-            send_sem=pr_s.at[q], recv_sem=pr_r.at[q], device_id=(z, partner), device_id_type=MESH)
-        cp.start()
-        pair.append(cp)
-
-    def from_partner(q):
-        pair[q].wait_recv()
-        pown[:, :, :, panel(q)] += prec[:, :, :, panel(q)]
+        put(ppar, q, part(1 - e, q))
+        for n in ((0,), (1,), (2, 3))[q]:
+            cp = pltpu.make_async_remote_copy(
+                src_ref=ppar[n], dst_ref=prec[n],
+                send_sem=pr_s.at[n], recv_sem=pr_r.at[n], device_id=(z, partner), device_id_type=MESH)
+            cp.start()
+            pair.append(cp)
+
+    def from_partner(n):
+        pair[n].wait_recv()
+        pown[n][...] += prec[n][...]
 
     def exchange(src, rec, send, recv, d, to, n=0):
         cp = pltpu.make_async_remote_copy(
@@ -264,11 +268,11 @@
     mid_of, end_of, second = [], [], [[], [], [], []]
 
     def open_stream(n):
-        lo, hi = STREAMS[n]
+        from_partner(n)
         if n % 2 == 0:
-            r = relay(lambda q, h: pown.at[2 * h:2 * h + 2, q, :, lo:hi], recs[n], rel_s, rel_r, x, *xn, base=6 * n)
+            r = relay(lambda q, h: pown[n].at[2 * h:2 * h + 2, q], recs[n], rel_s, rel_r, x, *xn, base=6 * n)
         else:
-            r = relay(lambda q, h: pown.at[q, 2 * h:2 * h + 2, :, lo:hi], recs[n], rel_s, rel_r, y, *yn, base=6 * n)
+            r = relay(lambda q, h: pown[n].at[q, 2 * h:2 * h + 2], recs[n], rel_s, rel_r, y, *yn, base=6 * n)
         mid_of.append((r[1], r[0]))
         end_of.append(r[2])
 
@@ -290,19 +294,16 @@
 
     arrived(0)
     to_partner(0)
-    pown[:, :, :, panel(0)] = part(e, 0)
+    put(pown, 0, part(e, 0))
     arrived(1)
     to_partner(1)
-    from_partner(0)
     open_stream(0)
-    pown[:, :, :, panel(1)] = part(e, 1)
+    put(pown, 1, part(e, 1))
     arrived(2)
     to_partner(2)
-    from_partner(1)
     open_stream(1)
-    pown[:, :, :, panel(2)] = part(e, 2)
+    put(pown, 2, part(e, 2))
     mid_of[0][0]()
-    from_partner(2)
     open_stream(2)
     open_stream(3)
     mid_of[1][0]()
@@ -314,12 +315,13 @@
     second_stage(3)
     def add(i, right, left):
         val = tmm(jnp.concatenate(right, axis=0), jnp.concatenate(left, axis=0))
-        phi[i] += val.reshape(4, 4, 2, 8, W)
+        for side in range(2):
+            phi[i, side] += val.reshape(4, 4, 2, 8, W)[:, :, side]
 
     def pair_terms(n):
         at = pl.ds(*SETS[n])
         cp = pltpu.make_async_remote_copy(
-            src_ref=phi.at[at, :, :, 1 - e], dst_ref=qrec.at[at],
+            src_ref=phi.at[at, 1 - e], dst_ref=qrec.at[at],
             send_sem=q_s.at[n], recv_sem=q_r.at[n], device_id=(z, partner), device_id_type=MESH)
         cp.start()
         return cp
@@ -330,7 +332,7 @@
     def met(n):
         terms[n].wait_recv()
         at = slice(SETS[n][0], SETS[n][0] + SETS[n][1])
-        qrec[at] += phi[at, :, :, e]
+        qrec[at] += phi[at, e]
 
     def spots(n, first_stage):
         along_x = GROUPS[n][4] == first_stage
@@ -475,21 +477,19 @@
             pltpu.VMEM((16, 2, 32, 512), BF16),
             pltpu.VMEM((16, 3, ROWS, W), BF16),
             pltpu.VMEM((3, 16, ROWS, W), BF16),
-            pltpu.VMEM((4, 4, ROWS, 768), F32),
-            pltpu.VMEM((4, 4, ROWS, 768), F32),
-            pltpu.VMEM((4, 4, ROWS, 768), F32),
+            *[[pltpu.VMEM((4, 4, ROWS, hi - lo), F32) for lo, hi in STREAMS]] * 3,
             *[pltpu.VMEM((6, 2, ROWS, hi - lo), F32) for lo, hi in STREAMS],
             *[pltpu.VMEM((3, ROWS, hi - lo), F32) for lo, hi in STREAMS],
             *[pltpu.VMEM((4, ROWS, hi - lo), F32) for lo, hi in STREAMS],
             pltpu.VMEM((ROWS, 768), F32),
-            pltpu.VMEM((6, 4, 4, 2, 8, W), F32),
+            pltpu.VMEM((6, 2, 4, 4, 8, W), F32),
             pltpu.VMEM((6, 4, 4, 8, W), F32),
             pltpu.VMEM((16, 8, 128), F32),
             pltpu.VMEM((15, 8, 128), F32),
             [pltpu.VMEM(shape, F32) for n, (_, nb, lo, hi, _) in enumerate(GROUPS) for shape in (
                 (3, nb, 4, 8, hi - lo) if n else (6, nb, 2, 8, hi - lo), (3, nb, 8, hi - lo), (nb, 4, 8, hi - lo))],
             dma((6,)), pltpu.SemaphoreType.REGULAR,
-            dma((24,)), dma((24,)), dma((21,)), dma((21,)), dma((48,)), dma((48,)), dma((3,)), dma((3,)),
+            dma((24,)), dma((24,)), dma((21,)), dma((21,)), dma((48,)), dma((48,)), dma((4,)), dma((4,)),
             dma((24,)), dma((24,)), dma((12,)), dma((12,)),
             dma((3,)), dma((3,)), dma((18,)), dma((18,)), dma((15,)), dma((15,)), dma((15,)), dma((15,)),
         ],

time: 79.6 us -> 79.7 us (level)
  no operation moved by 1% of the time
where the time goes in v6:
time: 79.7 us; the launch traced here: 79.4 us
  Pallas kernels  78.8 us (99%)
    pallas_call x1, Pallas kernels, body(): pl.pallas_call(kernel, out_shape=(jax.ShapeDtypeStruct((3, ROWS, W), F32)...  77.2 us

profile of v6, /device:TPU:1, one launch (start us, length us, event | category | flops | bytes accessed | tf_op | source)
XLA Modules:
  0.0 79.4 jit_solution(5663777225059481508)
XLA Ops:
  0.6 77.2 %chain_inverse.1 = (f32[3,32,256]{2,1,0:T(8,128)}, f32[8,128]{1,0:T(8,128)}) custom-call(f32[1024,512]{1,0:T(8,128)} %a_hbm.1, bf16[32,256]{1,0:T(8,128)(2,1)} %p1.1, bf16[32,256]{1,0:T(8,128)(2,1)} %p2.1, bf16[32,256]{1,0:T(8,128)(2,1)} %p3.1, bf16[3,256,256]{2,1,0:T(8,128)(2,1)} %coup_hbm.1, f32[3,256,256]{2,1,0:T(8,128)} %diag_hbm.1, s32[1,60]{1,0:T(1,128)} %bitcast.3, ...), custom_call_target="tpu_custom_call" | custom-call | tf_op jit(solution)/shard_map/chain_inverse/pallas_call | solution.py:464
  77.9 1.6 %hand_out.1 = (f32[32,256]{1,0:T(8,128)}, f32[32,256]{1,0:T(8,128)}, f32[32,256]{1,0:T(8,128)}, f32[6,8,16]{2,1,0:T(8,128)}) custom-call(f32[3,32,256]{2,1,0:T(8,128)} %get-tuple-element.10.blocks, f32[8,128]{1,0:T(8,128)} %get-tuple-element.11.tile), custom_call_target="tpu_custom_call" | custom-call | tf_op jit(solution)/shard_map/hand_out/pallas_call | solution.py:504

commit v7 on v6

--- a/solution.py
+++ b/solution.py
@@ -15,7 +15,7 @@
 GROUPS = (
     (0, 3, 0, 256, True), (3, 2, 0, 128, True), (3, 2, 128, 256, False), (5, 1, 0, 128, True), (5, 1, 128, 256, False),
 )
-SETS = ((0, 3), (3, 2), (5, 1))
+SETS = ((0, 3), (3, 2))
 STREAMS = ((0, 256), (256, 512), (512, 640), (640, 768))
 
 
@@ -58,10 +58,10 @@
     o, ot,
     a_vm, coup, diag, ahi, alo, ring, fbuf, pown, ppar, prec,
     rec0, rec1, rec2, rec3, far0, far1, far2, far3, mid0, mid1, mid2, mid3, ysum,
-    phi, qrec, zsend, zrec, gr,
-    lsem, in_sem, up_s, up_r, dn_s, dn_r, f_s, f_r, pr_s, pr_r,
+    phi, qrec, zsend, zrec, gr, o_vm,
+    lsem, o_sem, in_sem, up_s, up_r, dn_s, dn_r, f_s, f_r, pr_s, pr_r,
     rel_s, rel_r, far_s, far_r,
-    q_s, q_r, g_s, g_r, gf_s, gf_r, z_s, z_r,
+    q_s, q_r, last_s, last_r, g_s, g_r, gf_s, gf_r, z_s, z_r,
 ):
     z = lax.axis_index("row")
     c = lax.axis_index("col")
@@ -354,6 +354,32 @@
         return [exchange(group_mid[n].at[:, to[d][0]], group_far[n], gf_s, gf_r, d, to[d][1], n=3 * n)
                 for d in (2, 1, 3)]
 
+    def open_last(n):
+        to = spots(n, True)
+        lo, hi, xfirst = GROUPS[n][2:]
+        cps = []
+        for d, flip in ((2, 0), (2, 1), (1, 0), (3, 0), (1, 1), (3, 1), (0, 1)):
+            side = (e + flip) % 2
+            src = phi.at[5, side, :, to[d][0], :, lo:hi] if xfirst else phi.at[5, side, to[d][0], :, :, lo:hi]
+            at = 2 * d + flip - 1
+            cp = pltpu.make_async_remote_copy(
+                src_ref=src, dst_ref=group_rec[n].at[at],
+                send_sem=last_s.at[7 * (n - 3) + at], recv_sem=last_r.at[7 * (n - 3) + at],
+                device_id=(z, to[d][1] - e + side), device_id_type=MESH)
+            cp.start()
+            cps.append(cp)
+        return cps
+
+    def turn_last(n, cps):
+        for cp in cps:
+            cp.wait_recv()
+        lo, hi, xfirst = GROUPS[n][2:]
+        val = phi[5, e, :, x, :, lo:hi] if xfirst else phi[5, e, y, :, :, lo:hi]
+        for at in range(7):
+            val = val + group_rec[n][at]
+        group_mid[n][0] = val
+        return second_group(n)
+
     def turn_direct(n, cps):
         for cp in cps:
             cp.wait_recv()
@@ -372,6 +398,14 @@
             for i in range(val.shape[0]):
                 at = 16 * (blk + i)
                 zsend[zz, :, at:at + 16] = val[i][:, 16 * zz:16 * zz + 16]
+
+    gave = []
+
+    def give(n, val):
+        o_vm[n] = val
+        cp = pltpu.make_async_copy(o_vm.at[n], o.at[n], o_sem.at[n])
+        cp.start()
+        gave.append(cp)
 
     terms = []
     close_stream(0)
@@ -383,14 +417,14 @@
     add(1, [f2, -a], [y1, f1])
     add(2, [f3 - h, u - w], [y1, f1])
     terms.append(pair_terms(0))
-    o[0] = -y1
+    give(0, -y1)
     close_stream(1)
     y2 = (ysum[:, W:2 * W] - a) * keep2
     v = mm(y2, c2)
     add(3, [y2, -f2, a], [f2, a, b])
     add(4, [f3, -(w + v), g + h, -u], [y2, f2, a, b])
     terms.append(pair_terms(1))
-    o[1] = -y2
+    give(1, -y2)
     met(0)
     wide, wide_mid, wide_end = relay(
         lambda q, hh: qrec.at[0:3, 2 * hh:2 * hh + 2, q], ga_rec, g_s, g_r, x, *xn)
@@ -400,19 +434,19 @@
     close_stream(3)
     y3 = (ysum[:, 2 * W:3 * W] - w - v) * keep3
     add(5, [y3, h - f3, w - u, -f3, w + v, -(g + h), u], [f3, w, g, v, h, u, q_])
-    terms.append(pair_terms(2))
-    o[2] = -y3
+    firsts, lasts = {}, {}
+    for n in (3, 4):
+        firsts[n] = open_last(n)
+    give(2, -y3)
     met(1)
-    firsts, lasts = {}, {}
     for n in (1, 2):
         firsts[n] = open_direct(n)
     wide_mid()
-    met(2)
-    for n in (3, 4):
-        firsts[n] = open_direct(n)
     ga_mid[:, 0:2], ga_mid[:, 2:4] = wide_end()
     lasts[0] = second_group(0)
-    for n in (1, 2, 3, 4):
+    for n in (3, 4):
+        lasts[n] = turn_last(n, firsts[n])
+    for n in (1, 2):
         lasts[n] = turn_direct(n, firsts[n])
     pack(0, close_group(0, lasts[0]))
     for n, blk in ((1, 3), (3, 5)):
@@ -434,6 +468,8 @@
         tile = tile + zrec[d]
     ot[...] = tile
 
+    for cp in gave:
+        cp.wait()
     for way in (1, -1):
         for dist in range(1, REACH[way] + 1):
             for q in range(3):
@@ -468,7 +504,7 @@
             jax.ShapeDtypeStruct((8, 128), F32),
         ),
         in_specs=[any_spec] * 6 + [vm] * 2,
-        out_specs=(vm,) * 2,
+        out_specs=(any_spec, vm),
         scratch_shapes=[
             pltpu.VMEM((1024, 512), F32),
             pltpu.VMEM((3, W, W), BF16),
@@ -483,15 +519,16 @@
             *[pltpu.VMEM((4, ROWS, hi - lo), F32) for lo, hi in STREAMS],
             pltpu.VMEM((ROWS, 768), F32),
             pltpu.VMEM((6, 2, 4, 4, 8, W), F32),
-            pltpu.VMEM((6, 4, 4, 8, W), F32),
+            pltpu.VMEM((5, 4, 4, 8, W), F32),
             pltpu.VMEM((16, 8, 128), F32),
             pltpu.VMEM((15, 8, 128), F32),
             [pltpu.VMEM(shape, F32) for n, (_, nb, lo, hi, _) in enumerate(GROUPS) for shape in (
-                (3, nb, 4, 8, hi - lo) if n else (6, nb, 2, 8, hi - lo), (3, nb, 8, hi - lo), (nb, 4, 8, hi - lo))],
-            dma((6,)), pltpu.SemaphoreType.REGULAR,
+                ((6, nb, 2, 8, hi - lo), (3, nb, 4, 8, hi - lo), (7, 4, 8, hi - lo))[min(2, (n + 1) // 2)], (3, nb, 8, hi - lo), (nb, 4, 8, hi - lo))],
+            pltpu.VMEM((3, ROWS, W), F32),
+            dma((6,)), dma((3,)), pltpu.SemaphoreType.REGULAR,
             dma((24,)), dma((24,)), dma((21,)), dma((21,)), dma((48,)), dma((48,)), dma((4,)), dma((4,)),
             dma((24,)), dma((24,)), dma((12,)), dma((12,)),
-            dma((3,)), dma((3,)), dma((18,)), dma((18,)), dma((15,)), dma((15,)), dma((15,)), dma((15,)),
+            dma((2,)), dma((2,)), dma((14,)), dma((14,)), dma((12,)), dma((12,)), dma((15,)), dma((15,)), dma((15,)), dma((15,)),
         ],
         compiler_params=pltpu.CompilerParams(
             collective_id=0, has_side_effects=True, vmem_limit_bytes=56 << 20

time: 79.7 us -> 80.6 us (1.011)
  Pallas kernels: 78.8 us -> 79.7 us
    pallas_call x1, Pallas kernels: 77.2 us -> 78.1 us  [body(): pl.pallas_call(kernel, out_shape=(jax.ShapeDtypeStruct((3, ROWS, W), F32)...]
where the time goes in v7:
time: 80.6 us; the launch traced here: 80.4 us
  Pallas kernels  79.7 us (99%)
    pallas_call x1, Pallas kernels, body(): pl.pallas_call(kernel, out_shape=(jax.ShapeDtypeStruct((3, ROWS, W), F32)...  78.1 us

profile of v7, /device:TPU:1, one launch (start us, length us, event | category | flops | bytes accessed | tf_op | source)
XLA Modules:
  0.0 80.4 jit_solution(14365409221214808084)
XLA Ops:
  0.6 78.1 %chain_inverse.1 = (f32[3,32,256]{2,1,0:T(8,128)}, f32[8,128]{1,0:T(8,128)}) custom-call(f32[1024,512]{1,0:T(8,128)} %a_hbm.1, bf16[32,256]{1,0:T(8,128)(2,1)} %p1.1, bf16[32,256]{1,0:T(8,128)(2,1)} %p2.1, bf16[32,256]{1,0:T(8,128)(2,1)} %p3.1, bf16[3,256,256]{2,1,0:T(8,128)(2,1)} %coup_hbm.1, f32[3,256,256]{2,1,0:T(8,128)} %diag_hbm.1, s32[1,60]{1,0:T(1,128)} %bitcast.3, ...), custom_call_target="tpu_custom_call" | custom-call | tf_op jit(solution)/shard_map/chain_inverse/pallas_call | solution.py:500
  78.8 1.6 %hand_out.1 = (f32[32,256]{1,0:T(8,128)}, f32[32,256]{1,0:T(8,128)}, f32[32,256]{1,0:T(8,128)}, f32[6,8,16]{2,1,0:T(8,128)}) custom-call(f32[3,32,256]{2,1,0:T(8,128)} %get-tuple-element.10.blocks, f32[8,128]{1,0:T(8,128)} %get-tuple-element.11.tile), custom_call_target="tpu_custom_call" | custom-call | tf_op jit(solution)/shard_map/hand_out/pallas_call | solution.py:541

commit v8 on v6

--- a/solution.py
+++ b/solution.py
@@ -307,9 +307,9 @@
     open_stream(2)
     open_stream(3)
     mid_of[1][0]()
-    second_stage(0)
     mid_of[2][0]()
     mid_of[3][0]()
+    second_stage(0)
     second_stage(1)
     second_stage(2)
     second_stage(3)

time: 79.7 us -> 80.2 us (level)
  no operation moved by 1% of the time
where the time goes in v8:
time: 80.2 us; the launch traced here: 80 us
  Pallas kernels  79.3 us (99%)
    pallas_call x1, Pallas kernels, body(): pl.pallas_call(kernel, out_shape=(jax.ShapeDtypeStruct((3, ROWS, W), F32)...  77.8 us

profile of v8, /device:TPU:1, one launch (start us, length us, event | category | flops | bytes accessed | tf_op | source)
XLA Modules:
  0.0 80.0 jit_solution(4435996187670042349)
XLA Ops:
  0.6 77.8 %chain_inverse.1 = (f32[3,32,256]{2,1,0:T(8,128)}, f32[8,128]{1,0:T(8,128)}) custom-call(f32[1024,512]{1,0:T(8,128)} %a_hbm.1, bf16[32,256]{1,0:T(8,128)(2,1)} %p1.1, bf16[32,256]{1,0:T(8,128)(2,1)} %p2.1, bf16[32,256]{1,0:T(8,128)(2,1)} %p3.1, bf16[3,256,256]{2,1,0:T(8,128)(2,1)} %coup_hbm.1, f32[3,256,256]{2,1,0:T(8,128)} %diag_hbm.1, s32[1,60]{1,0:T(1,128)} %bitcast.3, ...), custom_call_target="tpu_custom_call" | custom-call | tf_op jit(solution)/shard_map/chain_inverse/pallas_call | solution.py:464
  78.4 1.6 %hand_out.1 = (f32[32,256]{1,0:T(8,128)}, f32[32,256]{1,0:T(8,128)}, f32[32,256]{1,0:T(8,128)}, f32[6,8,16]{2,1,0:T(8,128)}) custom-call(f32[3,32,256]{2,1,0:T(8,128)} %get-tuple-element.10.blocks, f32[8,128]{1,0:T(8,128)} %get-tuple-element.11.tile), custom_call_target="tpu_custom_call" | custom-call | tf_op jit(solution)/shard_map/hand_out/pallas_call | solution.py:504

commit v9 on v6

--- a/solution.py
+++ b/solution.py
@@ -58,8 +58,8 @@
     o, ot,
     a_vm, coup, diag, ahi, alo, ring, fbuf, pown, ppar, prec,
     rec0, rec1, rec2, rec3, far0, far1, far2, far3, mid0, mid1, mid2, mid3, ysum,
-    phi, qrec, zsend, zrec, gr,
-    lsem, in_sem, up_s, up_r, dn_s, dn_r, f_s, f_r, pr_s, pr_r,
+    phi, qrec, zsend, zrec, gr, o_vm,
+    lsem, o_sem, in_sem, up_s, up_r, dn_s, dn_r, f_s, f_r, pr_s, pr_r,
     rel_s, rel_r, far_s, far_r,
     q_s, q_r, g_s, g_r, gf_s, gf_r, z_s, z_r,
 ):
@@ -373,6 +373,14 @@
                 at = 16 * (blk + i)
                 zsend[zz, :, at:at + 16] = val[i][:, 16 * zz:16 * zz + 16]
 
+    gave = []
+
+    def give(n, val):
+        o_vm[n] = val
+        cp = pltpu.make_async_copy(o_vm.at[n], o.at[n], o_sem.at[n])
+        cp.start()
+        gave.append(cp)
+
     terms = []
     close_stream(0)
     y1 = ysum[:, 0:W]
@@ -383,14 +391,14 @@
     add(1, [f2, -a], [y1, f1])
     add(2, [f3 - h, u - w], [y1, f1])
     terms.append(pair_terms(0))
-    o[0] = -y1
+    give(0, -y1)
     close_stream(1)
     y2 = (ysum[:, W:2 * W] - a) * keep2
     v = mm(y2, c2)
     add(3, [y2, -f2, a], [f2, a, b])
     add(4, [f3, -(w + v), g + h, -u], [y2, f2, a, b])
     terms.append(pair_terms(1))
-    o[1] = -y2
+    give(1, -y2)
     met(0)
     wide, wide_mid, wide_end = relay(
         lambda q, hh: qrec.at[0:3, 2 * hh:2 * hh + 2, q], ga_rec, g_s, g_r, x, *xn)
@@ -401,7 +409,7 @@
     y3 = (ysum[:, 2 * W:3 * W] - w - v) * keep3
     add(5, [y3, h - f3, w - u, -f3, w + v, -(g + h), u], [f3, w, g, v, h, u, q_])
     terms.append(pair_terms(2))
-    o[2] = -y3
+    give(2, -y3)
     met(1)
     firsts, lasts = {}, {}
     for n in (1, 2):
@@ -434,6 +442,8 @@
         tile = tile + zrec[d]
     ot[...] = tile
 
+    for cp in gave:
+        cp.wait()
     for way in (1, -1):
         for dist in range(1, REACH[way] + 1):
             for q in range(3):
@@ -468,7 +478,7 @@
             jax.ShapeDtypeStruct((8, 128), F32),
         ),
         in_specs=[any_spec] * 6 + [vm] * 2,
-        out_specs=(vm,) * 2,
+        out_specs=(any_spec, vm),
         scratch_shapes=[
             pltpu.VMEM((1024, 512), F32),
             pltpu.VMEM((3, W, W), BF16),
@@ -488,7 +498,8 @@
             pltpu.VMEM((15, 8, 128), F32),
             [pltpu.VMEM(shape, F32) for n, (_, nb, lo, hi, _) in enumerate(GROUPS) for shape in (
                 (3, nb, 4, 8, hi - lo) if n else (6, nb, 2, 8, hi - lo), (3, nb, 8, hi - lo), (nb, 4, 8, hi - lo))],
-            dma((6,)), pltpu.SemaphoreType.REGULAR,
+            pltpu.VMEM((3, ROWS, W), F32),
+            dma((6,)), dma((3,)), pltpu.SemaphoreType.REGULAR,
             dma((24,)), dma((24,)), dma((21,)), dma((21,)), dma((48,)), dma((48,)), dma((4,)), dma((4,)),
             dma((24,)), dma((24,)), dma((12,)), dma((12,)),
             dma((3,)), dma((3,)), dma((18,)), dma((18,)), dma((15,)), dma((15,)), dma((15,)), dma((15,)),

time: 79.7 us -> 79.7 us (level)
  no operation moved by 1% of the time
where the time goes in v9:
time: 79.7 us; the launch traced here: 79.4 us
  Pallas kernels  78.8 us (99%)
    pallas_call x1, Pallas kernels, body(): pl.pallas_call(kernel, out_shape=(jax.ShapeDtypeStruct((3, ROWS, W), F32)...  77.2 us

profile of v9, /device:TPU:1, one launch (start us, length us, event | category | flops | bytes accessed | tf_op | source)
XLA Modules:
  0.0 79.4 jit_solution(3089341186313505076)
XLA Ops:
  0.6 77.2 %chain_inverse.1 = (f32[3,32,256]{2,1,0:T(8,128)}, f32[8,128]{1,0:T(8,128)}) custom-call(f32[1024,512]{1,0:T(8,128)} %a_hbm.1, bf16[32,256]{1,0:T(8,128)(2,1)} %p1.1, bf16[32,256]{1,0:T(8,128)(2,1)} %p2.1, bf16[32,256]{1,0:T(8,128)(2,1)} %p3.1, bf16[3,256,256]{2,1,0:T(8,128)(2,1)} %coup_hbm.1, f32[3,256,256]{2,1,0:T(8,128)} %diag_hbm.1, s32[1,60]{1,0:T(1,128)} %bitcast.3, ...), custom_call_target="tpu_custom_call" | custom-call | tf_op jit(solution)/shard_map/chain_inverse/pallas_call | solution.py:474
  77.9 1.6 %hand_out.1 = (f32[32,256]{1,0:T(8,128)}, f32[32,256]{1,0:T(8,128)}, f32[32,256]{1,0:T(8,128)}, f32[6,8,16]{2,1,0:T(8,128)}) custom-call(f32[3,32,256]{2,1,0:T(8,128)} %get-tuple-element.10.blocks, f32[8,128]{1,0:T(8,128)} %get-tuple-element.11.tile), custom_call_target="tpu_custom_call" | custom-call | tf_op jit(solution)/shard_map/hand_out/pallas_call | solution.py:515
